TPU v7x, 256 devices: a whole 4x4x8 slice. The times are simulated.
256 devices in a mesh: pb: 16 (over z, x_hi), kv: 16 (over x_lo, y, core).
Axes of the slice: x: 4 (x_hi: 2, x_lo: 2; x = x_hi * 2 + x_lo), y: 4, z: 8, core: 2. Of those that a mesh axis runs over, the one named last changes fastest.
Arguments:
- queries: bfloat16 [32768, 1024], P(('pb', 'kv')), may hold values from -6 to 6
- key_rows: bfloat16 [32768, 128], P(('pb', 'kv')), may hold values from -6 to 6
- value_rows: bfloat16 [32768, 128], P(('pb', 'kv')), may hold values from -6 to 6
- out_grad: bfloat16 [32768, 1024], P(('pb', 'kv')), may hold values from -6 to 6
- doc_ids: int32 [256], replicated, may hold values from 0 to 63, never falling along the last dimension, each value on 1 to 16 neighbouring positions
Outputs:
- attended: bfloat16 [32768, 1024], P(('pb', 'kv'))
- query_grad: bfloat16 [32768, 1024], P(('pb', 'kv'))
- key_grad: bfloat16 [32768, 128], P(('pb', 'kv'))
- value_grad: bfloat16 [32768, 128], P(('pb', 'kv'))
Inputs may be any that keep to these rules, and one draw needn't show every extreme that they name: `doc_ids`: ids never fall along the sequence; each document covers 1 to 16 consecutive blocks, and one covers exactly 16.
All inputs are finite; a program needn't handle non-finite values.
Results may differ from a plain program's by a relative error of at most 0.03.
Values may be sent and summed in bfloat16 or wider, within the bound.
A program may use at most 64 MiB of HBM per device.

v0:
```python
import jax
import jax.numpy as jnp
from jax import lax
from jax.sharding import PartitionSpec as P

HEADS = 8
HEAD_DIM = 128
BLOCK = 128


NEG_FILL = -1e30


def passed_along(block, axis, distance):
    devices = range(lax.axis_size(axis))
    route = [(i - distance, i) for i in devices if i - distance in devices]
    return lax.ppermute(block, axis, route)


def shifted(shard, axis, by):
    length = lax.axis_size(axis)
    return lax.ppermute(shard, axis, [(i, (i + by) % length) for i in range(length)])


def contract_last(left, right):
    return lax.dot_general(
        left, right, (((1,), (1,)), ((), ())), preferred_element_type=jnp.float32
    )


def contract_first(left, right):
    return lax.dot_general(
        left, right, (((0,), (0,)), ((), ())), preferred_element_type=jnp.float32
    )


def tile_mask(doc_ids, query_dev, key_dev, row_count):
    per_dev = row_count // BLOCK
    query_docs = jnp.repeat(
        lax.dynamic_slice_in_dim(doc_ids, query_dev * per_dev, per_dev, 0), BLOCK
    )
    key_docs = jnp.repeat(
        lax.dynamic_slice_in_dim(doc_ids, jnp.maximum(key_dev, 0) * per_dev, per_dev, 0), BLOCK
    )
    local_pos = jnp.arange(row_count, dtype=jnp.int32)
    query_pos = query_dev * row_count + local_pos
    key_pos = key_dev * row_count + local_pos
    allowed = (
        (query_docs[:, None] == key_docs[None, :])
        & (key_pos[None, :] <= query_pos[:, None])
        & (key_dev >= 0)
    )
    return jnp.repeat(allowed, HEADS, axis=0)


def local(queries, key_rows, value_rows, out_grad, doc_ids):
    row_count = queries.shape[0]
    flat_rows = row_count * HEADS
    cycle_len = lax.axis_size("kv")
    column = lax.axis_index("kv")
    query_dev = lax.axis_index("pb") * cycle_len + column
    score_scale = HEAD_DIM ** (-0.5)
    query_flat = queries.reshape(flat_rows, HEAD_DIM)
    grad_flat = out_grad.reshape(flat_rows, HEAD_DIM)
    kv_pair = jnp.stack([key_rows, value_rows])
    offsets = jnp.arange(cycle_len, dtype=jnp.int32)

    def cycle_column(offset):
        return (column - offset) % cycle_len

    def tile_scores(kv_shard, allowed):
        return jnp.where(allowed, contract_last(query_flat, kv_shard[0]) * score_scale, NEG_FILL)

    def absorb(softmax_stats, offset, kv_shard):
        allowed = tile_mask(doc_ids, query_dev, query_dev - offset, row_count)
        running_max, running_sum = softmax_stats
        scores = tile_scores(kv_shard, allowed)
        new_max = jnp.maximum(running_max, jnp.max(scores, axis=1))
        fresh = jnp.sum(jnp.where(allowed, jnp.exp(scores - new_max[:, None]), 0.0), axis=1)
        return (new_max, running_sum * jnp.exp(running_max - new_max) + fresh)

    start_stats = (
        jnp.full((flat_rows,), NEG_FILL, jnp.float32),
        jnp.zeros((flat_rows,), jnp.float32),
    )
    behind = passed_along(kv_pair, "pb", 1)

    def pick_shard(bundles, offset):
        return jnp.where(cycle_column(offset) <= column, bundles[0], bundles[1])

    def forward_turn(running, offset):
        bundles, softmax_stats = running
        kv_shard = pick_shard(bundles, offset)
        softmax_stats = absorb(softmax_stats, offset, kv_shard)
        bundles = shifted(bundles, "kv", 1)
        return ((bundles, softmax_stats), kv_shard)

    final_run, stored = lax.scan(
        forward_turn, (jnp.stack([kv_pair, behind]), start_stats), offsets[:-1]
    )
    bundles, softmax_stats = final_run
    last_shard = pick_shard(bundles, cycle_len - 1)
    softmax_stats = absorb(softmax_stats, cycle_len - 1, last_shard)
    stored = jnp.concatenate([stored, last_shard[None]], axis=0)
    row_max, row_sum = softmax_stats
    log_total = row_max + jnp.log(row_sum)

    def weights_for(scores, allowed):
        return jnp.where(allowed, jnp.exp(scores - log_total[:, None]), 0.0)

    def emit(mixed_rows, inputs):
        offset, kv_shard = inputs
        allowed = tile_mask(doc_ids, query_dev, query_dev - offset, row_count)
        weights = weights_for(tile_scores(kv_shard, allowed), allowed)
        return (
            mixed_rows
            + jnp.dot(
                weights.astype(jnp.bfloat16), kv_shard[1], preferred_element_type=jnp.float32
            ),
            None,
        )

    mixed_rows = lax.scan(emit, jnp.zeros((flat_rows, HEAD_DIM), jnp.float32), (offsets, stored))[0]
    attended = mixed_rows.reshape(row_count, HEADS * HEAD_DIM).astype(jnp.bfloat16)
    delta_rows = jnp.sum(
        grad_flat.astype(jnp.float32) * attended.reshape(flat_rows, HEAD_DIM).astype(jnp.float32),
        axis=1,
    )
    query_zero = jnp.zeros((flat_rows, HEAD_DIM), jnp.float32)

    def contribution(offset, kv_shard):
        allowed = tile_mask(doc_ids, query_dev, query_dev - offset, row_count)
        weights = weights_for(tile_scores(kv_shard, allowed), allowed)
        weights_b = weights.astype(jnp.bfloat16)
        grad_probs = contract_last(grad_flat, kv_shard[1])
        score_grad = (score_scale * weights * (grad_probs - delta_rows[:, None])).astype(
            jnp.bfloat16
        )
        query_part = jnp.dot(score_grad, kv_shard[0], preferred_element_type=jnp.float32)
        pair_part = jnp.stack(
            [contract_first(score_grad, query_flat), contract_first(weights_b, grad_flat)]
        )
        return (query_part, pair_part)

    def backward_turn(running, inputs):
        carried, query_acc = running
        query_part, pair_part = contribution(inputs[0], inputs[1])
        own_side = cycle_column(inputs[0]) <= column
        carried = carried + jnp.stack(
            [jnp.where(own_side, pair_part, 0.0), jnp.where(own_side, 0.0, pair_part)]
        )
        carried = shifted(carried, "kv", 1)
        return ((carried, query_acc + query_part), None)

    start_carry = jnp.zeros((2, 2, row_count, HEAD_DIM), jnp.float32)
    carried, query_acc = lax.scan(backward_turn, (start_carry, query_zero), (offsets, stored))[0]
    ahead = passed_along(carried[1], "pb", -1)
    pair_grad = carried[0] + ahead
    query_grad = query_acc.reshape(row_count, HEADS * HEAD_DIM).astype(jnp.bfloat16)
    return (
        attended,
        query_grad,
        pair_grad[0].astype(jnp.bfloat16),
        pair_grad[1].astype(jnp.bfloat16),
    )


def solution(mesh):
    in_specs = (
        P(("pb", "kv"), None),
        P(("pb", "kv"), None),
        P(("pb", "kv"), None),
        P(("pb", "kv"), None),
        P(),
    )
    out_specs = (
        P(("pb", "kv"), None),
        P(("pb", "kv"), None),
        P(("pb", "kv"), None),
        P(("pb", "kv"), None),
    )
    return jax.shard_map(local, mesh=mesh, in_specs=in_specs, out_specs=out_specs, check_vma=False)
```

profile of v0, /device:TPU:102, one launch (start us, length us, event | category | flops | bytes accessed | tf_op | source)
XLA Modules:
  0.0 395.9 jit_solution(6033365856825556245)
XLA Ops:
  0.6 0.8 fusion.37
  1.5 5.9 %collective-permute-start.2 = (bf16[2,128,128]{2,1,0:T(8,128)(2,1)S(1)}, bf16[2,128,128]{2,1,0:T(8,128)(2,1)S(1)}, u32[]{:S(2)}, u32[]{:S(2)}) collective-permute-start(bf16[2,128,128]{2,1,0:T(8,128)(2,1)S(1)} %get-tuple-element.632), channel_id=1, source_target_pairs={{0,16},{16,32},{32,48},{48,64},{64,80},{80,96},{96,112},{112,128},... | collective-permute-start | bytes 196616 | tf_op jit(solution)/shard_map/ppermute | solution.py:17
  7.4 1.4 fusion.39
  10.4 0.8 copy-done.2
  11.6 0.7 copy-done.3
  12.3 98.9 %while.47 = (s32[]{:T(128)}, bf16[2,2,128,128]{3,2,1,0:T(8,128)(2,1)S(1)}, f32[1024]{0:T(1024)S(1)}, f32[1024]{0:T(1024)S(1)}, bf16[15,2,128,128]{3,2,1,0:T(8,12...) while((s32[]{:T(128)}, ...), condition=%wide.region_3.4_spmd.clone, body=%wide.region_0.3_spmd.clone.sunk | while | flops 34428180 | bytes 3135927 | solution.py:98
  14.3 0.6 dynamic_slice.82
  17.0 1.9 collective-permute-done
  20.9 0.6 dynamic_slice.82
  23.6 1.9 collective-permute-done
  27.5 0.6 dynamic_slice.82
  30.2 1.9 collective-permute-done
  36.8 1.9 collective-permute-done
  43.4 1.9 collective-permute-done
  50.0 1.9 collective-permute-done
  56.6 1.9 collective-permute-done
  63.1 1.9 collective-permute-done
  69.7 1.9 collective-permute-done
  76.3 1.9 collective-permute-done
  82.9 1.9 collective-permute-done
  89.5 1.9 collective-permute-done
  96.1 1.9 collective-permute-done
  102.7 1.9 collective-permute-done
  109.3 1.9 collective-permute-done
  111.7 0.9 copy-done
  112.6 59.6 %while.48 = (s32[]{:T(128)}, f32[1024,128]{1,0:T(8,128)S(1)}, s32[16]{0:T(128)S(1)}, s32[]{:T(128)}, s32[256]{0:T(256)S(1)}, /*index=5*/s32[1]{0:T(128)}, s32[]{...) while((s32[]{:T(128)}, f32[1024,128]{1,0:T(8,128)S(1)}, ...), condition=%wide.region_7.8_spmd.clone, body=%wide.region_6.7_spmd.clone.sunk | while | flops 68075784 | bytes 1417466 | solution.py:123
  172.5 212.3 %while.49 = (s32[]{:T(128)}, f32[2,2,128,128]{3,2,1,0:T(8,128)S(1)}, f32[1024,128]{1,0:T(8,128)S(1)}, s32[16]{0:T(128)S(1)}, s32[]{:T(128)}, /*index=5*/s32[]{:T...) while((s32[]{:T(128)}, ...), condition=%wide.region_10.11_spmd.clone, body=%wide.region_9.10_spmd.clone.sunk | while | flops 169492736 | bytes 7481830 | solution.py:156
  178.2 7.6 %collective-permute-done.1 = f32[2,2,128,128]{3,2,1,0:T(8,128)S(1)} collective-permute-done((f32[2,2,128,128]{3,2,1,0:T(8,128)S(1)}, f32[2,2,128,128]{3,2,1,0:T(8,128)S(1)}, u32[]{:S(2)}, u32[]{:S(2)}) %collective-permute-start.1) | collective-permute-done | bytes 262176 | tf_op jit(solution)/shard_map/while/body/eval_jaxpr/ppermute | solution.py:22
  191.4 7.6 %collective-permute-done.1 = f32[2,2,128,128]{3,2,1,0:T(8,128)S(1)} collective-permute-done((f32[2,2,128,128]{3,2,1,0:T(8,128)S(1)}, f32[2,2,128,128]{3,2,1,0:T(8,128)S(1)}, u32[]{:S(2)}, u32[]{:S(2)}) %collective-permute-start.1) | collective-permute-done | bytes 262176 | tf_op jit(solution)/shard_map/while/body/eval_jaxpr/ppermute | solution.py:22
  204.6 7.6 %collective-permute-done.1 = f32[2,2,128,128]{3,2,1,0:T(8,128)S(1)} collective-permute-done((f32[2,2,128,128]{3,2,1,0:T(8,128)S(1)}, f32[2,2,128,128]{3,2,1,0:T(8,128)S(1)}, u32[]{:S(2)}, u32[]{:S(2)}) %collective-permute-start.1) | collective-permute-done | bytes 262176 | tf_op jit(solution)/shard_map/while/body/eval_jaxpr/ppermute | solution.py:22
  217.8 7.6 %collective-permute-done.1 = f32[2,2,128,128]{3,2,1,0:T(8,128)S(1)} collective-permute-done((f32[2,2,128,128]{3,2,1,0:T(8,128)S(1)}, f32[2,2,128,128]{3,2,1,0:T(8,128)S(1)}, u32[]{:S(2)}, u32[]{:S(2)}) %collective-permute-start.1) | collective-permute-done | bytes 262176 | tf_op jit(solution)/shard_map/while/body/eval_jaxpr/ppermute | solution.py:22
  231.1 7.6 %collective-permute-done.1 = f32[2,2,128,128]{3,2,1,0:T(8,128)S(1)} collective-permute-done((f32[2,2,128,128]{3,2,1,0:T(8,128)S(1)}, f32[2,2,128,128]{3,2,1,0:T(8,128)S(1)}, u32[]{:S(2)}, u32[]{:S(2)}) %collective-permute-start.1) | collective-permute-done | bytes 262176 | tf_op jit(solution)/shard_map/while/body/eval_jaxpr/ppermute | solution.py:22
  244.3 7.6 %collective-permute-done.1 = f32[2,2,128,128]{3,2,1,0:T(8,128)S(1)} collective-permute-done((f32[2,2,128,128]{3,2,1,0:T(8,128)S(1)}, f32[2,2,128,128]{3,2,1,0:T(8,128)S(1)}, u32[]{:S(2)}, u32[]{:S(2)}) %collective-permute-start.1) | collective-permute-done | bytes 262176 | tf_op jit(solution)/shard_map/while/body/eval_jaxpr/ppermute | solution.py:22
  257.5 7.6 %collective-permute-done.1 = f32[2,2,128,128]{3,2,1,0:T(8,128)S(1)} collective-permute-done((f32[2,2,128,128]{3,2,1,0:T(8,128)S(1)}, f32[2,2,128,128]{3,2,1,0:T(8,128)S(1)}, u32[]{:S(2)}, u32[]{:S(2)}) %collective-permute-start.1) | collective-permute-done | bytes 262176 | tf_op jit(solution)/shard_map/while/body/eval_jaxpr/ppermute | solution.py:22
  270.8 7.6 %collective-permute-done.1 = f32[2,2,128,128]{3,2,1,0:T(8,128)S(1)} collective-permute-done((f32[2,2,128,128]{3,2,1,0:T(8,128)S(1)}, f32[2,2,128,128]{3,2,1,0:T(8,128)S(1)}, u32[]{:S(2)}, u32[]{:S(2)}) %collective-permute-start.1) | collective-permute-done | bytes 262176 | tf_op jit(solution)/shard_map/while/body/eval_jaxpr/ppermute | solution.py:22
  284.0 7.6 %collective-permute-done.1 = f32[2,2,128,128]{3,2,1,0:T(8,128)S(1)} collective-permute-done((f32[2,2,128,128]{3,2,1,0:T(8,128)S(1)}, f32[2,2,128,128]{3,2,1,0:T(8,128)S(1)}, u32[]{:S(2)}, u32[]{:S(2)}) %collective-permute-start.1) | collective-permute-done | bytes 262176 | tf_op jit(solution)/shard_map/while/body/eval_jaxpr/ppermute | solution.py:22
  297.2 7.6 %collective-permute-done.1 = f32[2,2,128,128]{3,2,1,0:T(8,128)S(1)} collective-permute-done((f32[2,2,128,128]{3,2,1,0:T(8,128)S(1)}, f32[2,2,128,128]{3,2,1,0:T(8,128)S(1)}, u32[]{:S(2)}, u32[]{:S(2)}) %collective-permute-start.1) | collective-permute-done | bytes 262176 | tf_op jit(solution)/shard_map/while/body/eval_jaxpr/ppermute | solution.py:22
  310.5 7.6 %collective-permute-done.1 = f32[2,2,128,128]{3,2,1,0:T(8,128)S(1)} collective-permute-done((f32[2,2,128,128]{3,2,1,0:T(8,128)S(1)}, f32[2,2,128,128]{3,2,1,0:T(8,128)S(1)}, u32[]{:S(2)}, u32[]{:S(2)}) %collective-permute-start.1) | collective-permute-done | bytes 262176 | tf_op jit(solution)/shard_map/while/body/eval_jaxpr/ppermute | solution.py:22
  323.7 7.6 %collective-permute-done.1 = f32[2,2,128,128]{3,2,1,0:T(8,128)S(1)} collective-permute-done((f32[2,2,128,128]{3,2,1,0:T(8,128)S(1)}, f32[2,2,128,128]{3,2,1,0:T(8,128)S(1)}, u32[]{:S(2)}, u32[]{:S(2)}) %collective-permute-start.1) | collective-permute-done | bytes 262176 | tf_op jit(solution)/shard_map/while/body/eval_jaxpr/ppermute | solution.py:22
  336.9 7.6 %collective-permute-done.1 = f32[2,2,128,128]{3,2,1,0:T(8,128)S(1)} collective-permute-done((f32[2,2,128,128]{3,2,1,0:T(8,128)S(1)}, f32[2,2,128,128]{3,2,1,0:T(8,128)S(1)}, u32[]{:S(2)}, u32[]{:S(2)}) %collective-permute-start.1) | collective-permute-done | bytes 262176 | tf_op jit(solution)/shard_map/while/body/eval_jaxpr/ppermute | solution.py:22
  350.1 7.6 %collective-permute-done.1 = f32[2,2,128,128]{3,2,1,0:T(8,128)S(1)} collective-permute-done((f32[2,2,128,128]{3,2,1,0:T(8,128)S(1)}, f32[2,2,128,128]{3,2,1,0:T(8,128)S(1)}, u32[]{:S(2)}, u32[]{:S(2)}) %collective-permute-start.1) | collective-permute-done | bytes 262176 | tf_op jit(solution)/shard_map/while/body/eval_jaxpr/ppermute | solution.py:22
  363.4 7.6 %collective-permute-done.1 = f32[2,2,128,128]{3,2,1,0:T(8,128)S(1)} collective-permute-done((f32[2,2,128,128]{3,2,1,0:T(8,128)S(1)}, f32[2,2,128,128]{3,2,1,0:T(8,128)S(1)}, u32[]{:S(2)}, u32[]{:S(2)}) %collective-permute-start.1) | collective-permute-done | bytes 262176 | tf_op jit(solution)/shard_map/while/body/eval_jaxpr/ppermute | solution.py:22
  376.6 8.2 %collective-permute-done.1 = f32[2,2,128,128]{3,2,1,0:T(8,128)S(1)} collective-permute-done((f32[2,2,128,128]{3,2,1,0:T(8,128)S(1)}, f32[2,2,128,128]{3,2,1,0:T(8,128)S(1)}, u32[]{:S(2)}, u32[]{:S(2)}) %collective-permute-start.1) | collective-permute-done | bytes 262176 | tf_op jit(solution)/shard_map/while/body/eval_jaxpr/ppermute | solution.py:22
  384.8 1.9 collective-permute-start.3
  386.7 0.8 convert_element_type.45
  387.5 0.8 convert_element_type.49
  388.4 6.9 %collective-permute-done.3 = f32[2,128,128]{2,1,0:T(8,128)S(1)} collective-permute-done((f32[2,128,128]{2,1,0:T(8,128)S(1)}, f32[2,128,128]{2,1,0:T(8,128)S(1)}, u32[]{:S(2)}, u32[]{:S(2)}) %collective-permute-start.3) | collective-permute-done | bytes 131104 | tf_op jit(solution)/shard_map/ppermute | solution.py:17
  395.3 0.6 slice_bitcast_fusion.3
  (558 shorter events, 106.4 us)
Async XLA Ops:
  0.6 9.6 %copy-start.1 = (bf16[128,1024]{1,0:T(8,128)(2,1)S(1)}, bf16[128,1024]{1,0:T(8,128)(2,1)}, u32[]{:S(2)}) copy-start(bf16[128,1024]{1,0:T(8,128)(2,1)} %param.14) | copy-start | bytes 786436
  1.5 10.1 %collective-permute-start.2 = (bf16[2,128,128]{2,1,0:T(8,128)(2,1)S(1)}, bf16[2,128,128]{2,1,0:T(8,128)(2,1)S(1)}, u32[]{:S(2)}, u32[]{:S(2)}) collective-permute-start(bf16[2,128,128]{2,1,0:T(8,128)(2,1)S(1)} %get-tuple-element.632), channel_id=1, source_target_pairs={{0,16},{16,32},{32,48},{48,64},{64,80},{80,96},{96,112},{112,128},... | collective-permute-start | bytes 196616 | tf_op jit(solution)/shard_map/ppermute | solution.py:17
  10.3 1.0 copy-start.2
  11.6 0.7 copy-start.3
  12.3 6.6 %collective-permute-start = (bf16[2,2,128,128]{3,2,1,0:T(8,128)(2,1)S(1)}, bf16[2,2,128,128]{3,2,1,0:T(8,128)(2,1)S(1)}, u32[]{:S(2)}, u32[]{:S(2)}) collective-permute-start(bf16[2,2,128,128]{3,2,1,0:T(8,128)(2,1)S(1)} %copy.26), channel_id=1, source_target_pairs={{0,1},{1,2},{2,3},{3,4},{4,5},{5,6},{6,7},{7,8},{8,9},{9,10},{10,1... | collective-permute-start | bytes 393224 | tf_op jit(solution)/shard_map/while/body/eval_jaxpr/ppermute | solution.py:22
  18.9 6.6 %collective-permute-start = (bf16[2,2,128,128]{3,2,1,0:T(8,128)(2,1)S(1)}, bf16[2,2,128,128]{3,2,1,0:T(8,128)(2,1)S(1)}, u32[]{:S(2)}, u32[]{:S(2)}) collective-permute-start(bf16[2,2,128,128]{3,2,1,0:T(8,128)(2,1)S(1)} %copy.26), channel_id=1, source_target_pairs={{0,1},{1,2},{2,3},{3,4},{4,5},{5,6},{6,7},{7,8},{8,9},{9,10},{10,1... | collective-permute-start | bytes 393224 | tf_op jit(solution)/shard_map/while/body/eval_jaxpr/ppermute | solution.py:22
  25.5 6.6 %collective-permute-start = (bf16[2,2,128,128]{3,2,1,0:T(8,128)(2,1)S(1)}, bf16[2,2,128,128]{3,2,1,0:T(8,128)(2,1)S(1)}, u32[]{:S(2)}, u32[]{:S(2)}) collective-permute-start(bf16[2,2,128,128]{3,2,1,0:T(8,128)(2,1)S(1)} %copy.26), channel_id=1, source_target_pairs={{0,1},{1,2},{2,3},{3,4},{4,5},{5,6},{6,7},{7,8},{8,9},{9,10},{10,1... | collective-permute-start | bytes 393224 | tf_op jit(solution)/shard_map/while/body/eval_jaxpr/ppermute | solution.py:22
  32.1 6.6 %collective-permute-start = (bf16[2,2,128,128]{3,2,1,0:T(8,128)(2,1)S(1)}, bf16[2,2,128,128]{3,2,1,0:T(8,128)(2,1)S(1)}, u32[]{:S(2)}, u32[]{:S(2)}) collective-permute-start(bf16[2,2,128,128]{3,2,1,0:T(8,128)(2,1)S(1)} %copy.26), channel_id=1, source_target_pairs={{0,1},{1,2},{2,3},{3,4},{4,5},{5,6},{6,7},{7,8},{8,9},{9,10},{10,1... | collective-permute-start | bytes 393224 | tf_op jit(solution)/shard_map/while/body/eval_jaxpr/ppermute | solution.py:22
  38.7 6.6 %collective-permute-start = (bf16[2,2,128,128]{3,2,1,0:T(8,128)(2,1)S(1)}, bf16[2,2,128,128]{3,2,1,0:T(8,128)(2,1)S(1)}, u32[]{:S(2)}, u32[]{:S(2)}) collective-permute-start(bf16[2,2,128,128]{3,2,1,0:T(8,128)(2,1)S(1)} %copy.26), channel_id=1, source_target_pairs={{0,1},{1,2},{2,3},{3,4},{4,5},{5,6},{6,7},{7,8},{8,9},{9,10},{10,1... | collective-permute-start | bytes 393224 | tf_op jit(solution)/shard_map/while/body/eval_jaxpr/ppermute | solution.py:22
  45.3 6.6 %collective-permute-start = (bf16[2,2,128,128]{3,2,1,0:T(8,128)(2,1)S(1)}, bf16[2,2,128,128]{3,2,1,0:T(8,128)(2,1)S(1)}, u32[]{:S(2)}, u32[]{:S(2)}) collective-permute-start(bf16[2,2,128,128]{3,2,1,0:T(8,128)(2,1)S(1)} %copy.26), channel_id=1, source_target_pairs={{0,1},{1,2},{2,3},{3,4},{4,5},{5,6},{6,7},{7,8},{8,9},{9,10},{10,1... | collective-permute-start | bytes 393224 | tf_op jit(solution)/shard_map/while/body/eval_jaxpr/ppermute | solution.py:22
  51.9 6.6 %collective-permute-start = (bf16[2,2,128,128]{3,2,1,0:T(8,128)(2,1)S(1)}, bf16[2,2,128,128]{3,2,1,0:T(8,128)(2,1)S(1)}, u32[]{:S(2)}, u32[]{:S(2)}) collective-permute-start(bf16[2,2,128,128]{3,2,1,0:T(8,128)(2,1)S(1)} %copy.26), channel_id=1, source_target_pairs={{0,1},{1,2},{2,3},{3,4},{4,5},{5,6},{6,7},{7,8},{8,9},{9,10},{10,1... | collective-permute-start | bytes 393224 | tf_op jit(solution)/shard_map/while/body/eval_jaxpr/ppermute | solution.py:22
  58.5 6.6 %collective-permute-start = (bf16[2,2,128,128]{3,2,1,0:T(8,128)(2,1)S(1)}, bf16[2,2,128,128]{3,2,1,0:T(8,128)(2,1)S(1)}, u32[]{:S(2)}, u32[]{:S(2)}) collective-permute-start(bf16[2,2,128,128]{3,2,1,0:T(8,128)(2,1)S(1)} %copy.26), channel_id=1, source_target_pairs={{0,1},{1,2},{2,3},{3,4},{4,5},{5,6},{6,7},{7,8},{8,9},{9,10},{10,1... | collective-permute-start | bytes 393224 | tf_op jit(solution)/shard_map/while/body/eval_jaxpr/ppermute | solution.py:22
  65.0 6.6 %collective-permute-start = (bf16[2,2,128,128]{3,2,1,0:T(8,128)(2,1)S(1)}, bf16[2,2,128,128]{3,2,1,0:T(8,128)(2,1)S(1)}, u32[]{:S(2)}, u32[]{:S(2)}) collective-permute-start(bf16[2,2,128,128]{3,2,1,0:T(8,128)(2,1)S(1)} %copy.26), channel_id=1, source_target_pairs={{0,1},{1,2},{2,3},{3,4},{4,5},{5,6},{6,7},{7,8},{8,9},{9,10},{10,1... | collective-permute-start | bytes 393224 | tf_op jit(solution)/shard_map/while/body/eval_jaxpr/ppermute | solution.py:22
  71.6 6.6 %collective-permute-start = (bf16[2,2,128,128]{3,2,1,0:T(8,128)(2,1)S(1)}, bf16[2,2,128,128]{3,2,1,0:T(8,128)(2,1)S(1)}, u32[]{:S(2)}, u32[]{:S(2)}) collective-permute-start(bf16[2,2,128,128]{3,2,1,0:T(8,128)(2,1)S(1)} %copy.26), channel_id=1, source_target_pairs={{0,1},{1,2},{2,3},{3,4},{4,5},{5,6},{6,7},{7,8},{8,9},{9,10},{10,1... | collective-permute-start | bytes 393224 | tf_op jit(solution)/shard_map/while/body/eval_jaxpr/ppermute | solution.py:22
  78.2 6.6 %collective-permute-start = (bf16[2,2,128,128]{3,2,1,0:T(8,128)(2,1)S(1)}, bf16[2,2,128,128]{3,2,1,0:T(8,128)(2,1)S(1)}, u32[]{:S(2)}, u32[]{:S(2)}) collective-permute-start(bf16[2,2,128,128]{3,2,1,0:T(8,128)(2,1)S(1)} %copy.26), channel_id=1, source_target_pairs={{0,1},{1,2},{2,3},{3,4},{4,5},{5,6},{6,7},{7,8},{8,9},{9,10},{10,1... | collective-permute-start | bytes 393224 | tf_op jit(solution)/shard_map/while/body/eval_jaxpr/ppermute | solution.py:22
  84.8 6.6 %collective-permute-start = (bf16[2,2,128,128]{3,2,1,0:T(8,128)(2,1)S(1)}, bf16[2,2,128,128]{3,2,1,0:T(8,128)(2,1)S(1)}, u32[]{:S(2)}, u32[]{:S(2)}) collective-permute-start(bf16[2,2,128,128]{3,2,1,0:T(8,128)(2,1)S(1)} %copy.26), channel_id=1, source_target_pairs={{0,1},{1,2},{2,3},{3,4},{4,5},{5,6},{6,7},{7,8},{8,9},{9,10},{10,1... | collective-permute-start | bytes 393224 | tf_op jit(solution)/shard_map/while/body/eval_jaxpr/ppermute | solution.py:22
  91.4 6.6 %collective-permute-start = (bf16[2,2,128,128]{3,2,1,0:T(8,128)(2,1)S(1)}, bf16[2,2,128,128]{3,2,1,0:T(8,128)(2,1)S(1)}, u32[]{:S(2)}, u32[]{:S(2)}) collective-permute-start(bf16[2,2,128,128]{3,2,1,0:T(8,128)(2,1)S(1)} %copy.26), channel_id=1, source_target_pairs={{0,1},{1,2},{2,3},{3,4},{4,5},{5,6},{6,7},{7,8},{8,9},{9,10},{10,1... | collective-permute-start | bytes 393224 | tf_op jit(solution)/shard_map/while/body/eval_jaxpr/ppermute | solution.py:22
  98.0 6.6 %collective-permute-start = (bf16[2,2,128,128]{3,2,1,0:T(8,128)(2,1)S(1)}, bf16[2,2,128,128]{3,2,1,0:T(8,128)(2,1)S(1)}, u32[]{:S(2)}, u32[]{:S(2)}) collective-permute-start(bf16[2,2,128,128]{3,2,1,0:T(8,128)(2,1)S(1)} %copy.26), channel_id=1, source_target_pairs={{0,1},{1,2},{2,3},{3,4},{4,5},{5,6},{6,7},{7,8},{8,9},{9,10},{10,1... | collective-permute-start | bytes 393224 | tf_op jit(solution)/shard_map/while/body/eval_jaxpr/ppermute | solution.py:22
  104.6 6.6 %collective-permute-start = (bf16[2,2,128,128]{3,2,1,0:T(8,128)(2,1)S(1)}, bf16[2,2,128,128]{3,2,1,0:T(8,128)(2,1)S(1)}, u32[]{:S(2)}, u32[]{:S(2)}) collective-permute-start(bf16[2,2,128,128]{3,2,1,0:T(8,128)(2,1)S(1)} %copy.26), channel_id=1, source_target_pairs={{0,1},{1,2},{2,3},{3,4},{4,5},{5,6},{6,7},{7,8},{8,9},{9,10},{10,1... | collective-permute-start | bytes 393224 | tf_op jit(solution)/shard_map/while/body/eval_jaxpr/ppermute | solution.py:22
  111.6 1.0 copy-start
  177.7 8.0 %collective-permute-start.1 = (f32[2,2,128,128]{3,2,1,0:T(8,128)S(1)}, f32[2,2,128,128]{3,2,1,0:T(8,128)S(1)}, u32[]{:S(2)}, u32[]{:S(2)}) collective-permute-start(f32[2,2,128,128]{3,2,1,0:T(8,128)S(1)} %maximum_add_fusion.2), channel_id=1, source_target_pairs={{0,1},{1,2},{2,3},{3,4},{4,5},{5,6},{6,7},{7,8},{8,9},{9,10},{10,1... | collective-permute-start | bytes 786440 | tf_op jit(solution)/shard_map/while/body/eval_jaxpr/ppermute | solution.py:22
  191.0 8.0 %collective-permute-start.1 = (f32[2,2,128,128]{3,2,1,0:T(8,128)S(1)}, f32[2,2,128,128]{3,2,1,0:T(8,128)S(1)}, u32[]{:S(2)}, u32[]{:S(2)}) collective-permute-start(f32[2,2,128,128]{3,2,1,0:T(8,128)S(1)} %maximum_add_fusion.2), channel_id=1, source_target_pairs={{0,1},{1,2},{2,3},{3,4},{4,5},{5,6},{6,7},{7,8},{8,9},{9,10},{10,1... | collective-permute-start | bytes 786440 | tf_op jit(solution)/shard_map/while/body/eval_jaxpr/ppermute | solution.py:22
  204.2 8.0 %collective-permute-start.1 = (f32[2,2,128,128]{3,2,1,0:T(8,128)S(1)}, f32[2,2,128,128]{3,2,1,0:T(8,128)S(1)}, u32[]{:S(2)}, u32[]{:S(2)}) collective-permute-start(f32[2,2,128,128]{3,2,1,0:T(8,128)S(1)} %maximum_add_fusion.2), channel_id=1, source_target_pairs={{0,1},{1,2},{2,3},{3,4},{4,5},{5,6},{6,7},{7,8},{8,9},{9,10},{10,1... | collective-permute-start | bytes 786440 | tf_op jit(solution)/shard_map/while/body/eval_jaxpr/ppermute | solution.py:22
  217.4 8.0 %collective-permute-start.1 = (f32[2,2,128,128]{3,2,1,0:T(8,128)S(1)}, f32[2,2,128,128]{3,2,1,0:T(8,128)S(1)}, u32[]{:S(2)}, u32[]{:S(2)}) collective-permute-start(f32[2,2,128,128]{3,2,1,0:T(8,128)S(1)} %maximum_add_fusion.2), channel_id=1, source_target_pairs={{0,1},{1,2},{2,3},{3,4},{4,5},{5,6},{6,7},{7,8},{8,9},{9,10},{10,1... | collective-permute-start | bytes 786440 | tf_op jit(solution)/shard_map/while/body/eval_jaxpr/ppermute | solution.py:22
  230.7 8.0 %collective-permute-start.1 = (f32[2,2,128,128]{3,2,1,0:T(8,128)S(1)}, f32[2,2,128,128]{3,2,1,0:T(8,128)S(1)}, u32[]{:S(2)}, u32[]{:S(2)}) collective-permute-start(f32[2,2,128,128]{3,2,1,0:T(8,128)S(1)} %maximum_add_fusion.2), channel_id=1, source_target_pairs={{0,1},{1,2},{2,3},{3,4},{4,5},{5,6},{6,7},{7,8},{8,9},{9,10},{10,1... | collective-permute-start | bytes 786440 | tf_op jit(solution)/shard_map/while/body/eval_jaxpr/ppermute | solution.py:22
  243.9 8.0 %collective-permute-start.1 = (f32[2,2,128,128]{3,2,1,0:T(8,128)S(1)}, f32[2,2,128,128]{3,2,1,0:T(8,128)S(1)}, u32[]{:S(2)}, u32[]{:S(2)}) collective-permute-start(f32[2,2,128,128]{3,2,1,0:T(8,128)S(1)} %maximum_add_fusion.2), channel_id=1, source_target_pairs={{0,1},{1,2},{2,3},{3,4},{4,5},{5,6},{6,7},{7,8},{8,9},{9,10},{10,1... | collective-permute-start | bytes 786440 | tf_op jit(solution)/shard_map/while/body/eval_jaxpr/ppermute | solution.py:22
  257.1 8.0 %collective-permute-start.1 = (f32[2,2,128,128]{3,2,1,0:T(8,128)S(1)}, f32[2,2,128,128]{3,2,1,0:T(8,128)S(1)}, u32[]{:S(2)}, u32[]{:S(2)}) collective-permute-start(f32[2,2,128,128]{3,2,1,0:T(8,128)S(1)} %maximum_add_fusion.2), channel_id=1, source_target_pairs={{0,1},{1,2},{2,3},{3,4},{4,5},{5,6},{6,7},{7,8},{8,9},{9,10},{10,1... | collective-permute-start | bytes 786440 | tf_op jit(solution)/shard_map/while/body/eval_jaxpr/ppermute | solution.py:22
  270.4 8.0 %collective-permute-start.1 = (f32[2,2,128,128]{3,2,1,0:T(8,128)S(1)}, f32[2,2,128,128]{3,2,1,0:T(8,128)S(1)}, u32[]{:S(2)}, u32[]{:S(2)}) collective-permute-start(f32[2,2,128,128]{3,2,1,0:T(8,128)S(1)} %maximum_add_fusion.2), channel_id=1, source_target_pairs={{0,1},{1,2},{2,3},{3,4},{4,5},{5,6},{6,7},{7,8},{8,9},{9,10},{10,1... | collective-permute-start | bytes 786440 | tf_op jit(solution)/shard_map/while/body/eval_jaxpr/ppermute | solution.py:22
  283.6 8.0 %collective-permute-start.1 = (f32[2,2,128,128]{3,2,1,0:T(8,128)S(1)}, f32[2,2,128,128]{3,2,1,0:T(8,128)S(1)}, u32[]{:S(2)}, u32[]{:S(2)}) collective-permute-start(f32[2,2,128,128]{3,2,1,0:T(8,128)S(1)} %maximum_add_fusion.2), channel_id=1, source_target_pairs={{0,1},{1,2},{2,3},{3,4},{4,5},{5,6},{6,7},{7,8},{8,9},{9,10},{10,1... | collective-permute-start | bytes 786440 | tf_op jit(solution)/shard_map/while/body/eval_jaxpr/ppermute | solution.py:22
  296.8 8.0 %collective-permute-start.1 = (f32[2,2,128,128]{3,2,1,0:T(8,128)S(1)}, f32[2,2,128,128]{3,2,1,0:T(8,128)S(1)}, u32[]{:S(2)}, u32[]{:S(2)}) collective-permute-start(f32[2,2,128,128]{3,2,1,0:T(8,128)S(1)} %maximum_add_fusion.2), channel_id=1, source_target_pairs={{0,1},{1,2},{2,3},{3,4},{4,5},{5,6},{6,7},{7,8},{8,9},{9,10},{10,1... | collective-permute-start | bytes 786440 | tf_op jit(solution)/shard_map/while/body/eval_jaxpr/ppermute | solution.py:22
  310.0 8.0 %collective-permute-start.1 = (f32[2,2,128,128]{3,2,1,0:T(8,128)S(1)}, f32[2,2,128,128]{3,2,1,0:T(8,128)S(1)}, u32[]{:S(2)}, u32[]{:S(2)}) collective-permute-start(f32[2,2,128,128]{3,2,1,0:T(8,128)S(1)} %maximum_add_fusion.2), channel_id=1, source_target_pairs={{0,1},{1,2},{2,3},{3,4},{4,5},{5,6},{6,7},{7,8},{8,9},{9,10},{10,1... | collective-permute-start | bytes 786440 | tf_op jit(solution)/shard_map/while/body/eval_jaxpr/ppermute | solution.py:22
  323.3 8.0 %collective-permute-start.1 = (f32[2,2,128,128]{3,2,1,0:T(8,128)S(1)}, f32[2,2,128,128]{3,2,1,0:T(8,128)S(1)}, u32[]{:S(2)}, u32[]{:S(2)}) collective-permute-start(f32[2,2,128,128]{3,2,1,0:T(8,128)S(1)} %maximum_add_fusion.2), channel_id=1, source_target_pairs={{0,1},{1,2},{2,3},{3,4},{4,5},{5,6},{6,7},{7,8},{8,9},{9,10},{10,1... | collective-permute-start | bytes 786440 | tf_op jit(solution)/shard_map/while/body/eval_jaxpr/ppermute | solution.py:22
  336.5 8.0 %collective-permute-start.1 = (f32[2,2,128,128]{3,2,1,0:T(8,128)S(1)}, f32[2,2,128,128]{3,2,1,0:T(8,128)S(1)}, u32[]{:S(2)}, u32[]{:S(2)}) collective-permute-start(f32[2,2,128,128]{3,2,1,0:T(8,128)S(1)} %maximum_add_fusion.2), channel_id=1, source_target_pairs={{0,1},{1,2},{2,3},{3,4},{4,5},{5,6},{6,7},{7,8},{8,9},{9,10},{10,1... | collective-permute-start | bytes 786440 | tf_op jit(solution)/shard_map/while/body/eval_jaxpr/ppermute | solution.py:22
  349.7 8.0 %collective-permute-start.1 = (f32[2,2,128,128]{3,2,1,0:T(8,128)S(1)}, f32[2,2,128,128]{3,2,1,0:T(8,128)S(1)}, u32[]{:S(2)}, u32[]{:S(2)}) collective-permute-start(f32[2,2,128,128]{3,2,1,0:T(8,128)S(1)} %maximum_add_fusion.2), channel_id=1, source_target_pairs={{0,1},{1,2},{2,3},{3,4},{4,5},{5,6},{6,7},{7,8},{8,9},{9,10},{10,1... | collective-permute-start | bytes 786440 | tf_op jit(solution)/shard_map/while/body/eval_jaxpr/ppermute | solution.py:22
  363.0 8.0 %collective-permute-start.1 = (f32[2,2,128,128]{3,2,1,0:T(8,128)S(1)}, f32[2,2,128,128]{3,2,1,0:T(8,128)S(1)}, u32[]{:S(2)}, u32[]{:S(2)}) collective-permute-start(f32[2,2,128,128]{3,2,1,0:T(8,128)S(1)} %maximum_add_fusion.2), channel_id=1, source_target_pairs={{0,1},{1,2},{2,3},{3,4},{4,5},{5,6},{6,7},{7,8},{8,9},{9,10},{10,1... | collective-permute-start | bytes 786440 | tf_op jit(solution)/shard_map/while/body/eval_jaxpr/ppermute | solution.py:22
  376.2 8.6 %collective-permute-start.1 = (f32[2,2,128,128]{3,2,1,0:T(8,128)S(1)}, f32[2,2,128,128]{3,2,1,0:T(8,128)S(1)}, u32[]{:S(2)}, u32[]{:S(2)}) collective-permute-start(f32[2,2,128,128]{3,2,1,0:T(8,128)S(1)} %maximum_add_fusion.2), channel_id=1, source_target_pairs={{0,1},{1,2},{2,3},{3,4},{4,5},{5,6},{6,7},{7,8},{8,9},{9,10},{10,1... | collective-permute-start | bytes 786440 | tf_op jit(solution)/shard_map/while/body/eval_jaxpr/ppermute | solution.py:22
  384.8 10.5 %collective-permute-start.3 = (f32[2,128,128]{2,1,0:T(8,128)S(1)}, f32[2,128,128]{2,1,0:T(8,128)S(1)}, u32[]{:S(2)}, u32[]{:S(2)}) collective-permute-start(f32[2,128,128]{2,1,0:T(8,128)S(1)} %slice_bitcast_fusion.2), channel_id=1, source_target_pairs={{16,0},{32,16},{48,32},{64,48},{80,64},{96,80},{112,96},{128,112},... | collective-permute-start | bytes 393224 | tf_op jit(solution)/shard_map/ppermute | solution.py:17
where the time goes:
time: 399 us; the launch traced here: 396 us
  waiting for transfers between devices  157 us (39%)
  loops' own time  114 us (29%)
  local copies, waits for them, and re-layouts  70.5 us (18%)
  matrix products  32.3 us (8%)
  starting transfers between devices  10.4 us (3%)
  other arithmetic  9.63 us (2%)
    ppermute x31, waiting for transfers between devices, shifted(): lax.ppermute(shard, axis, [(i, (i + by) % length) for i in range(length)])  150 us
    another operation x1, loops' own time, local(): lax.scan(backward_turn, (start_carry, query_zero), (offsets, stored))[0]  43.2 us
    another operation x1, loops' own time, local(): lax.scan(forward_turn, (jnp.stack([kv_pair, behind]), start_stats), offse...  39.3 us
    another operation x1, loops' own time, local(): lax.scan(emit, jnp.zeros((flat_rows, HEAD_DIM), jnp.float32), (offsets, s...  31.5 us
    dynamic_slice x48, local copies, waits for them, and re-layouts, tile_mask(): lax.dynamic_slice_in_dim(doc_ids, jnp.maximum(key_dev, 0) * per_dev, per_...  29.1 us
    dynamic_slice x32, local copies, waits for them, and re-layouts, local(): lax.scan(emit, jnp.zeros((flat_rows, HEAD_DIM), jnp.float32), (offsets, s...  18.7 us
    dot_general x48, matrix products, contract_last(): lax.dot_general(left, right, (((1,), (1,)), ((), ())), preferred_element_...  12.6 us
    dynamic_slice x15, local copies, waits for them, and re-layouts, local(): lax.scan(forward_turn, (jnp.stack([kv_pair, behind]), start_stats), offse...  8.83 us
  transfers between devices with their start and end apart: 33, of which 32 were waited for; matrix products, arithmetic and copies ran while one was open for 10% of the time, Pallas kernels for 0%

commit v1 on v0

v1 whole, which is shorter than its diff:
```python
import jax
import jax.numpy as jnp
from jax import lax
from jax.experimental import pallas as pl
from jax.experimental.pallas import tpu as pltpu
from jax.sharding import PartitionSpec as P

HEADS = 8
HEAD_DIM = 128
BLOCK = 128
NBLK = 256
WIDE = HEADS * HEAD_DIM

NEG = -1e30
SCALE = HEAD_DIM ** (-0.5)
LOG2E = 1.4426950408889634
EXP_SCALE = SCALE * LOG2E

MESH = pl.DeviceIdType.MESH


def dot_nn(a, b):
    return lax.dot_general(a, b, (((1,), (0,)), ((), ())), preferred_element_type=jnp.float32)


def dot_nt(a, b):
    return lax.dot_general(a, b, (((1,), (1,)), ((), ())), preferred_element_type=jnp.float32)


def head_cols(h):
    return slice(h * HEAD_DIM, (h + 1) * HEAD_DIM)


def kernel(
    q_hbm, k_hbm, v_hbm, g_hbm, docs_hbm,
    att_hbm, dq_hbm, dk_hbm, dv_hbm,
    kv, q_in, g_in, qt, gt, probs, maxes, run_max, run_sum, out_acc, dq_acc, delta,
    w_scr, ds_scr, pg, r1r, r2s, r2r, r3s, r3r, att_out, dq_out, dkv_out, docs,
    local_sem, docs_sem,
    x_send, x_recv, y_send, p_send, p_recv,
    r1_send, r1_recv, r2_send, r2_recv, r3_send, r3_recv,
):
    pb = lax.axis_index("pb")
    kvi = lax.axis_index("kv")
    p = pb * 16 + kvi
    c = lax.rem(kvi, 2)
    y = lax.rem(lax.div(kvi, 2), 4)
    col_base = lax.div(kvi, 8) * 8

    def seq_dev(delta_p):
        t = lax.rem(p + delta_p + NBLK, NBLK)
        return (lax.div(t, 16), lax.rem(t, 16))

    def y_dev(k):
        return (pb, col_base + lax.rem(y + k, 4) * 2 + c)

    partner = (pb, kvi + 1 - 2 * c)
    wraps = [None] + [lax.div(y + k, 4) for k in (1, 2, 3)]

    barrier = pltpu.get_barrier_semaphore()
    peers = [seq_dev(8), seq_dev(16), seq_dev(-8), seq_dev(-16), y_dev(1), y_dev(2), y_dev(3), partner]
    for peer in peers:
        pl.semaphore_signal(barrier, inc=1, device_id=peer, device_id_type=MESH)

    own_k = pltpu.make_async_copy(k_hbm, kv.at[0, c, 0], local_sem.at[0])
    own_v = pltpu.make_async_copy(v_hbm, kv.at[0, c, 1], local_sem.at[1])
    own_k.start()
    own_v.start()
    docs_copy = pltpu.make_async_copy(docs_hbm, docs, docs_sem)
    docs_copy.start()
    q_copy = pltpu.make_async_copy(q_hbm, q_in, local_sem.at[2])
    g_copy = pltpu.make_async_copy(g_hbm, g_in, local_sem.at[3])
    q_copy.start()
    g_copy.start()
    own_k.wait()
    own_v.wait()
    pl.semaphore_wait(barrier, len(peers))

    def remote(src, dst, send_sem, recv_sem, dev):
        return pltpu.make_async_remote_copy(
            src_ref=src, dst_ref=dst, send_sem=send_sem, recv_sem=recv_sem,
            device_id=dev, device_id_type=MESH)

    def x_copy(i):
        return remote(kv.at[0, c], kv.at[4 * i, c], x_send.at[i], x_recv.at[4 * i], seq_dev(8 * i))

    def y_copy(k, second):
        wrap = wraps[k]
        e = k + 4 * second
        return remote(kv.at[4 * wrap + 4 * second, c], kv.at[e, c], y_send.at[e], x_recv.at[e], y_dev(k))

    def p_copy(e):
        return remote(kv.at[e, c], kv.at[e, c], p_send.at[e], p_recv.at[e], partner)

    def special_copy():
        return remote(kv.at[8 * c, c], kv.at[0, c], p_send.at[0], p_recv.at[0], partner)

    x_copy(1).start()
    for k in (1, 2, 3):
        @pl.when(wraps[k] == 0)
        def _():
            y_copy(k, 0).start()
    x_copy(2).start()

    q_copy.wait()
    for h in range(HEADS):
        qt[:, head_cols(h)] = q_in[:, head_cols(h)].T
    docs_copy.wait()
    my_doc = docs[p]

    def bias_of(idx):
        same = (docs[jnp.maximum(idx, 0)] == my_doc) & (idx >= 0)
        return jnp.where(same, 0.0, NEG).astype(jnp.float32)

    def forward(keys, values_t, slot, parts, first):
        for h in range(HEADS):
            cols = head_cols(h)
            s = dot_nn(keys, qt[:, cols])
            if first:
                key_at = lax.broadcasted_iota(jnp.int32, s.shape, 0)
                query_at = lax.broadcasted_iota(jnp.int32, s.shape, 1)
                s = jnp.where(key_at <= query_at, s, NEG)
            tops = []
            for lo, _, _, bias in parts:
                top = jnp.max(s[lo:lo + BLOCK], axis=0, keepdims=True) * EXP_SCALE
                tops.append(top if bias is None else top + bias)
            new_max = tops[0]
            for top in tops[1:]:
                new_max = jnp.maximum(new_max, top)
            if not first:
                old_max = run_max[:, cols]
                new_max = jnp.maximum(new_max, old_max)
                alpha = jnp.exp2(old_max - new_max)
            run_max[:, cols] = new_max
            total = None
            pieces = []
            for lo, at, parity, bias in parts:
                shift = -new_max if bias is None else bias - new_max
                piece = jnp.exp2(s[lo:lo + BLOCK] * EXP_SCALE + shift)
                part_sum = jnp.sum(piece, axis=0, keepdims=True)
                total = part_sum if total is None else total + part_sum
                piece = piece.astype(jnp.bfloat16)
                probs[slot, pl.ds(at, BLOCK), cols] = piece
                pieces.append(piece)
                maxes[slot, parity, :, cols] = new_max
            tile = pieces[0] if len(pieces) == 1 else jnp.concatenate(pieces, axis=0)
            mixed = dot_nn(values_t, tile)
            if first:
                run_sum[:, cols] = total
                out_acc[:, cols] = mixed
            else:
                run_sum[:, cols] = run_sum[:, cols] * alpha + total
                out_acc[:, cols] = out_acc[:, cols] * alpha + mixed

    c_rows = pl.multiple_of(c * BLOCK, BLOCK)
    o_rows = pl.multiple_of((1 - c) * BLOCK, BLOCK)
    forward(kv[0, c, 0], kv[0, c, 1].T, 0, [(0, c_rows, c, None)], True)

    x_copy(1).wait_recv()
    p_copy(4).start()
    for k in (1, 2, 3):
        @pl.when(wraps[k] == 0)
        def _():
            y_copy(k, 1).start()

        @pl.when(wraps[k] == 1)
        def _():
            y_copy(k, 0).start()
    x_copy(2).wait_recv()
    special_copy().start()
    for k in (1, 2, 3):
        @pl.when(wraps[k] == 1)
        def _():
            y_copy(k, 1).start()

    g_copy.wait()
    for h in range(HEADS):
        gt[:, head_cols(h)] = g_in[:, head_cols(h)].T

    def arrival(j):
        i = lax.div(j - 1, 2)
        k = 2 * i + 1 - 3 * lax.div(i, 2)
        return jnp.where(j == 0, 4, k + 4 * lax.rem(j + 1, 2))

    def y_wait(e):
        remote(kv.at[e, c], kv.at[e, c], y_send.at[e], x_recv.at[e], partner).wait_recv()

    def forward_step(j, carry):
        e = arrival(j)

        @pl.when(j < 6)
        def _():
            nxt = arrival(j + 1)
            y_wait(nxt)
            p_copy(nxt).start()

        remote(kv.at[e, c], kv.at[e, 1 - c], p_send.at[e], p_recv.at[e], partner).wait_recv()
        keys = kv[e, :, 0].reshape(2 * BLOCK, HEAD_DIM)
        values_t = kv[e, :, 1].reshape(2 * BLOCK, HEAD_DIM).T
        base = p - c - 2 * e
        forward(keys, values_t, e, [(0, 0, 0, bias_of(base)), (BLOCK, BLOCK, 1, bias_of(base + 1))], False)
        return carry

    lax.fori_loop(0, 7, forward_step, 0)

    special_copy().wait_recv()
    special_at = jnp.where(c == 0, p - 15, p - 1)
    forward(kv[0, 1 - c, 0], kv[0, 1 - c, 1].T, 0, [(0, o_rows, 1 - c, bias_of(special_at))], False)

    for h in range(HEADS):
        cols = head_cols(h)
        inv = 1.0 / run_sum[:, cols]
        att_t = (out_acc[:, cols] * inv).astype(jnp.bfloat16)
        att_out[:, cols] = att_t.T
        delta[:, cols] = jnp.sum(
            att_t.astype(jnp.float32) * gt[:, cols].astype(jnp.float32), axis=0, keepdims=True)
        run_sum[:, cols] = inv
    att_copy = pltpu.make_async_copy(att_out, att_hbm, local_sem.at[0])
    att_copy.start()

    dq_acc[...] = jnp.zeros_like(dq_acc)

    def backward(e):
        keys_t = kv[e, :, 0].reshape(2 * BLOCK, HEAD_DIM).T
        values = kv[e, :, 1].reshape(2 * BLOCK, HEAD_DIM)
        for h in range(HEADS):
            cols = head_cols(h)
            gp = dot_nn(values, gt[:, cols]) - delta[:, cols]
            for parity in (0, 1):
                rows = slice(parity * BLOCK, (parity + 1) * BLOCK)
                factor = jnp.exp2(maxes[e, parity, :, cols] - run_max[:, cols]) * run_sum[:, cols]
                w = probs[e, rows, cols].astype(jnp.float32) * factor
                w_scr[rows, cols] = w.astype(jnp.bfloat16)
                ds_scr[rows, cols] = (w * gp[rows]).astype(jnp.bfloat16)
        ds = ds_scr[...]
        dk_t = dot_nt(qt[...], ds)
        dv_t = dot_nt(gt[...], w_scr[...])
        for parity in (0, 1):
            rows = slice(parity * BLOCK, (parity + 1) * BLOCK)
            pg[e, parity, 0] = dk_t[:, rows].astype(jnp.bfloat16)
            pg[e, parity, 1] = dv_t[:, rows].astype(jnp.bfloat16)
        dq_acc[...] += dot_nn(keys_t, ds)

    def r1_copy(e):
        return remote(pg.at[e, 1 - c], r1r.at[e], r1_send.at[e], r1_recv.at[e], partner)

    def r2_copy(e, k):
        return remote(r2s.at[e], r2r.at[e], r2_send.at[e], r2_recv.at[e], y_dev(4 - k))

    def chip_sum(e):
        r1_copy(e).wait_recv()
        return pg[e, c].astype(jnp.float32) + r1r[e].astype(jnp.float32)

    def give_back(j):
        i = lax.div(j, 2)
        k = 2 - i + 3 * lax.div(i, 2)
        return k, k + 4 * lax.rem(j, 2)

    def pass_on(j):
        k, e = give_back(j)
        r2s[e] = chip_sum(e).astype(jnp.bfloat16)
        r2_copy(e, k).start()

    def backward_step(j, carry):
        _, e = give_back(j)
        backward(e)
        r1_copy(e).start()

        @pl.when(j > 0)
        def _():
            pass_on(j - 1)

        return carry

    lax.fori_loop(0, 6, backward_step, 0)
    backward(4)
    r1_copy(4).start()
    pass_on(5)
    backward(0)
    r1_copy(0).start()

    for h in range(HEADS):
        cols = head_cols(h)
        dq_out[:, cols] = (dq_acc[:, cols] * SCALE).astype(jnp.bfloat16).T
    dq_copy = pltpu.make_async_copy(dq_out, dq_hbm, local_sem.at[1])
    dq_copy.start()

    one_back = chip_sum(4)
    own = pg[0, c].astype(jnp.float32)
    two_back = jnp.zeros_like(own)
    r1_copy(0).wait_recv()
    special = r1r[0].astype(jnp.float32)
    own = own + jnp.where(c == 0, special, 0.0)
    two_back = two_back + jnp.where(c == 0, 0.0, special)
    for k in (2, 1, 3):
        r2_copy(k, k).wait_recv()
        near = r2r[k].astype(jnp.float32)
        r2_copy(k + 4, k).wait_recv()
        far = r2r[k + 4].astype(jnp.float32)
        wrapped = wraps[k] == 1
        own = own + jnp.where(wrapped, 0.0, near)
        one_back = one_back + jnp.where(wrapped, near, far)
        two_back = two_back + jnp.where(wrapped, far, 0.0)
    r3s[0] = one_back.astype(jnp.bfloat16)
    r3s[1] = two_back.astype(jnp.bfloat16)

    def r3_copy(i):
        return remote(r3s.at[i], r3r.at[i], r3_send.at[i], r3_recv.at[i], seq_dev(-8 * (i + 1)))

    r3_copy(1).start()
    r3_copy(0).start()

    x_copy(1).wait_send()
    x_copy(2).wait_send()
    special_copy().wait_send()
    for e in range(1, 8):
        p_copy(e).wait_send()
    for k in (1, 2, 3):
        for second in (0, 1):
            y_copy(k, second).wait_send()
            r2_copy(k + 4 * second, k).wait_send()
    for e in range(8):
        r1_copy(e).wait_send()
    att_copy.wait()
    dq_copy.wait()

    r3_copy(0).wait_recv()
    r3_copy(1).wait_recv()
    total = own + r3r[0].astype(jnp.float32) + r3r[1].astype(jnp.float32)
    dkv_out[0] = (total[0] * SCALE).T.astype(jnp.bfloat16)
    dkv_out[1] = total[1].T.astype(jnp.bfloat16)
    dk_copy = pltpu.make_async_copy(dkv_out.at[0], dk_hbm, local_sem.at[2])
    dv_copy = pltpu.make_async_copy(dkv_out.at[1], dv_hbm, local_sem.at[3])
    dk_copy.start()
    dv_copy.start()
    r3_copy(0).wait_send()
    r3_copy(1).wait_send()
    dk_copy.wait()
    dv_copy.wait()


def local(queries, key_rows, value_rows, out_grad, doc_ids):
    bf16, f32 = jnp.bfloat16, jnp.float32
    dma = pltpu.SemaphoreType.DMA
    any_space = pl.BlockSpec(memory_space=pl.ANY)
    pair = (2, BLOCK, HEAD_DIM)
    return pl.pallas_call(
        kernel,
        out_shape=(
            jax.ShapeDtypeStruct((BLOCK, WIDE), bf16),
            jax.ShapeDtypeStruct((BLOCK, WIDE), bf16),
            jax.ShapeDtypeStruct((BLOCK, HEAD_DIM), bf16),
            jax.ShapeDtypeStruct((BLOCK, HEAD_DIM), bf16),
        ),
        in_specs=[any_space] * 5,
        out_specs=(any_space,) * 4,
        scratch_shapes=[
            pltpu.VMEM((9, 2) + pair, bf16),
            pltpu.VMEM((BLOCK, WIDE), bf16),
            pltpu.VMEM((BLOCK, WIDE), bf16),
            pltpu.VMEM((HEAD_DIM, WIDE), bf16),
            pltpu.VMEM((HEAD_DIM, WIDE), bf16),
            pltpu.VMEM((8, 2 * BLOCK, WIDE), bf16),
            pltpu.VMEM((8, 2, 1, WIDE), f32),
            pltpu.VMEM((1, WIDE), f32),
            pltpu.VMEM((1, WIDE), f32),
            pltpu.VMEM((HEAD_DIM, WIDE), f32),
            pltpu.VMEM((HEAD_DIM, WIDE), f32),
            pltpu.VMEM((1, WIDE), f32),
            pltpu.VMEM((2 * BLOCK, WIDE), bf16),
            pltpu.VMEM((2 * BLOCK, WIDE), bf16),
            pltpu.VMEM((8, 2) + pair, bf16),
            pltpu.VMEM((8,) + pair, bf16),
            pltpu.VMEM((8,) + pair, bf16),
            pltpu.VMEM((8,) + pair, bf16),
            pltpu.VMEM((2,) + pair, bf16),
            pltpu.VMEM((2,) + pair, bf16),
            pltpu.VMEM((BLOCK, WIDE), bf16),
            pltpu.VMEM((BLOCK, WIDE), bf16),
            pltpu.VMEM(pair, bf16),
            pltpu.SMEM((NBLK,), jnp.int32),
            dma((4,)),
            dma,
            dma((3,)), dma((9,)), dma((8,)), dma((8,)), dma((8,)),
            dma((8,)), dma((8,)), dma((8,)), dma((8,)), dma((2,)), dma((2,)),
        ],
        compiler_params=pltpu.CompilerParams(collective_id=0, has_side_effects=True),
    )(queries, key_rows, value_rows, out_grad, doc_ids)


def solution(mesh):
    rows = P(("pb", "kv"), None)
    return jax.shard_map(
        local, mesh=mesh, in_specs=(rows, rows, rows, rows, P()),
        out_specs=(rows, rows, rows, rows), check_vma=False)
```

time: 399 us -> 45.3 us (0.11)
  the two profiles are of different devices: /device:TPU:102 before, /device:TPU:8 now
where the time goes in v1:
time: 45.3 us; the launch traced here: 45.1 us
  Pallas kernels  40.6 us (90%)
  local copies, waits for them, and re-layouts  3.86 us (9%)
  between operations  0.65 us (1%)
    pallas_call x1, Pallas kernels, local(): pl.pallas_call(kernel, out_shape=(jax.ShapeDtypeStruct((BLOCK, WIDE), bf1...  40.6 us
    unnamed x10, local copies, waits for them, and re-layouts  3.86 us

profile of v1, /device:TPU:8, one launch (start us, length us, event | category | flops | bytes accessed | tf_op | source)
XLA Modules:
  0.0 45.1 jit_solution(229186549124513188)
XLA Ops:
  0.6 40.6 %shard_map.84 = (bf16[128,1024]{1,0:T(8,128)(2,1)}, bf16[128,1024]{1,0:T(8,128)(2,1)}, bf16[128,128]{1,0:T(8,128)(2,1)}, bf16[128,128]{1,0:T(8,128)(2,1)}) custom-call(bf16[128,1024]{1,0:T(8,128)(2,1)} %q_hbm.1, bf16[128,128]{1,0:T(8,128)(2,1)} %k_hbm.1, bf16[128,128]{1,0:T(8,128)(2,1)} %v_hbm.1, bf16[128,1024]{1,0:T(8,128)(2,1)} %g_hbm.1, s32[256]{0:T(256)} %docs_hbm.1), custom_call_target="tpu_custom_call" | custom-call | tf_op jit(solution)/shard_map/pallas_call | solution.py:347
  41.2 0.0 copy-start
  41.2 1.7 %copy.13 = bf16[128,1024]{1,0:T(8,128)(2,1)} copy(bf16[128,1024]{1,0:T(8,128)(2,1)} %get-tuple-element.8) | data formatting | bytes 524288
  42.9 0.0 copy-done
  42.9 0.0 copy-start.2
  42.9 0.7 %copy.14 = bf16[128,1024]{1,0:T(8,128)(2,1)} copy(bf16[128,1024]{1,0:T(8,128)(2,1)S(1)} %copy-done) | data formatting | bytes 524288
  43.6 0.1 copy-done.2
  43.7 0.0 copy-start.1
  43.7 0.6 %copy.15 = bf16[128,128]{1,0:T(8,128)(2,1)} copy(bf16[128,128]{1,0:T(8,128)(2,1)S(1)} %copy-done.2) | data formatting | bytes 65536
  44.3 0.2 copy-done.1
  44.5 0.6 %copy.16 = bf16[128,128]{1,0:T(8,128)(2,1)} copy(bf16[128,128]{1,0:T(8,128)(2,1)S(1)} %copy-done.1) | data formatting | bytes 65536
Async XLA Ops:
  41.2 1.7 %copy-start = (bf16[128,1024]{1,0:T(8,128)(2,1)S(1)}, bf16[128,1024]{1,0:T(8,128)(2,1)}, u32[]{:S(2)}) copy-start(bf16[128,1024]{1,0:T(8,128)(2,1)} %get-tuple-element.9) | copy-start | bytes 786436
  42.9 0.8 %copy-start.2 = (bf16[128,128]{1,0:T(8,128)(2,1)S(1)}, bf16[128,128]{1,0:T(8,128)(2,1)}, u32[]{:S(2)}) copy-start(bf16[128,128]{1,0:T(8,128)(2,1)} %get-tuple-element.10) | copy-start | bytes 98308
  43.7 0.8 %copy-start.1 = (bf16[128,128]{1,0:T(8,128)(2,1)S(1)}, bf16[128,128]{1,0:T(8,128)(2,1)}, u32[]{:S(2)}) copy-start(bf16[128,128]{1,0:T(8,128)(2,1)} %get-tuple-element.11) | copy-start | bytes 98308

commit v2 on v1

v2 whole, which is shorter than its diff:
```python
import jax
import jax.numpy as jnp
from jax import lax
from jax.experimental import pallas as pl
from jax.experimental.pallas import tpu as pltpu
from jax.sharding import PartitionSpec as P

HEADS = 8
HEAD_DIM = 128
BLOCK = 128
NBLK = 256
WIDE = HEADS * HEAD_DIM

NEG = -1e30
SCALE = HEAD_DIM ** (-0.5)
LOG2E = 1.4426950408889634
EXP_SCALE = SCALE * LOG2E

MESH = pl.DeviceIdType.MESH
SEND_ORDER = (1, 2, 3, 4, 5, 6, 7)


def dot_nn(a, b):
    return lax.dot_general(a, b, (((1,), (0,)), ((), ())), preferred_element_type=jnp.float32)


def dot_nt(a, b):
    return lax.dot_general(a, b, (((1,), (1,)), ((), ())), preferred_element_type=jnp.float32)


def side_by_side(ref):
    return jnp.concatenate([ref[h] for h in range(HEADS)], axis=1)


def head_cols(h):
    return slice(h * HEAD_DIM, (h + 1) * HEAD_DIM)


def kernel(
    q_hbm, k_hbm, v_hbm, g_hbm, docs_hbm,
    att_out, dq_out, dkv_out,
    kv, q_in, g_in, qt, gt, probs, maxes, run_max, run_sum, out_acc, dq_acc, delta,
    w_scr, ds_scr, pg, r1r, r2s, r2r, r3s, r3b, r3r, total, docs,
    local_sem, q_sem, g_sem, docs_sem,
    kv_send, kv_recv, p_send, p_recv,
    r1_send, r1_recv, r2_send, r2_recv, r3_send, r3_recv,
):
    pb = lax.axis_index("pb")
    kvi = lax.axis_index("kv")
    p = pb * 16 + kvi
    c = lax.rem(kvi, 2)
    y = lax.rem(lax.div(kvi, 2), 4)

    def seq_dev(delta_p):
        t = lax.rem(p + delta_p + NBLK, NBLK)
        return (lax.div(t, 16), lax.rem(t, 16))

    partner = (pb, kvi + 1 - 2 * c)
    chip = lax.div(p, 2)
    column = lax.div(p, 8)

    def there(e):
        return (chip + e >= 0) & (chip + e < NBLK // 2)

    @pl.when(column < 2)
    def _():
        for e in range(1, 9):
            kv[e, c] = jnp.zeros((2, BLOCK, HEAD_DIM), jnp.bfloat16)

    barrier = pltpu.get_barrier_semaphore()
    peers = [e for d in range(1, 9) for e in (d, -d)]
    count = jnp.int32(1)
    pl.semaphore_signal(barrier, inc=1, device_id=partner, device_id_type=MESH)
    for e in peers:
        count = count + there(e).astype(jnp.int32)

        @pl.when(there(e))
        def _():
            pl.semaphore_signal(barrier, inc=1, device_id=seq_dev(2 * e), device_id_type=MESH)

    own_k = pltpu.make_async_copy(k_hbm, kv.at[0, c, 0], local_sem.at[0])
    own_v = pltpu.make_async_copy(v_hbm, kv.at[0, c, 1], local_sem.at[1])
    own_k.start()
    own_v.start()
    docs_copy = pltpu.make_async_copy(docs_hbm, docs, docs_sem)
    docs_copy.start()
    q_copies = [
        pltpu.make_async_copy(q_hbm.at[:, head_cols(h)], q_in.at[h], q_sem.at[h]) for h in range(HEADS)]
    g_copies = [
        pltpu.make_async_copy(g_hbm.at[:, head_cols(h)], g_in.at[h], g_sem.at[h]) for h in range(HEADS)]
    for copy in q_copies + g_copies:
        copy.start()
    own_k.wait()
    own_v.wait()
    pl.semaphore_wait(barrier, count)

    def remote(src, dst, send_sem, recv_sem, dev):
        return pltpu.make_async_remote_copy(
            src_ref=src, dst_ref=dst, send_sem=send_sem, recv_sem=recv_sem,
            device_id=dev, device_id_type=MESH)

    def straight(e):
        return y + e < 8

    def kv_copy(e, passed):
        src = kv.at[8 if passed else 0, c]
        return remote(src, kv.at[e, c], kv_send.at[e], kv_recv.at[e], seq_dev(2 * e - (16 if passed else 0)))

    def kv_wait(e):
        @pl.when(there(-e))
        def _():
            remote(kv.at[0, c], kv.at[e, c], kv_send.at[e], kv_recv.at[e], partner).wait_recv()

    def p_copy(e):
        return remote(kv.at[e, c], kv.at[e, c], p_send.at[e], p_recv.at[e], partner)

    def special_copy():
        return remote(kv.at[8 * c, c], kv.at[0, c], p_send.at[0], p_recv.at[0], partner)

    @pl.when(there(8))
    def _():
        kv_copy(8, False).start()

    for e in SEND_ORDER:
        @pl.when(straight(e) & there(e))
        def _():
            kv_copy(e, False).start()

    for h in range(HEADS):
        q_copies[h].wait()
        qt[h] = q_in[h].T
    docs_copy.wait()
    my_doc = docs[p]

    def bias_of(idx):
        same = (docs[jnp.maximum(idx, 0)] == my_doc) & (idx >= 0)
        return jnp.where(same, 0.0, NEG).astype(jnp.float32)

    def forward(keys, values_t, slot, parts, first):
        for h in range(HEADS):
            cols = head_cols(h)
            s = dot_nn(keys, qt[h])
            if first:
                key_at = lax.broadcasted_iota(jnp.int32, s.shape, 0)
                query_at = lax.broadcasted_iota(jnp.int32, s.shape, 1)
                s = jnp.where(key_at <= query_at, s, NEG)
            tops = []
            for lo, _, _, bias in parts:
                top = jnp.max(s[lo:lo + BLOCK], axis=0, keepdims=True) * EXP_SCALE
                tops.append(top if bias is None else top + bias)
            new_max = tops[0]
            for top in tops[1:]:
                new_max = jnp.maximum(new_max, top)
            if not first:
                old_max = run_max[:, cols]
                new_max = jnp.maximum(new_max, old_max)
                alpha = jnp.exp2(old_max - new_max)
            run_max[:, cols] = new_max
            total = None
            pieces = []
            for lo, at, parity, bias in parts:
                shift = -new_max if bias is None else bias - new_max
                piece = jnp.exp2(s[lo:lo + BLOCK] * EXP_SCALE + shift)
                part_sum = jnp.sum(piece, axis=0, keepdims=True)
                total = part_sum if total is None else total + part_sum
                piece = piece.astype(jnp.bfloat16)
                probs[slot, h, pl.ds(at, BLOCK)] = piece
                pieces.append(piece)
                maxes[slot, parity, :, cols] = new_max
            tile = pieces[0] if len(pieces) == 1 else jnp.concatenate(pieces, axis=0)
            mixed = dot_nn(values_t, tile)
            if first:
                run_sum[:, cols] = total
                out_acc[:, cols] = mixed
            else:
                run_sum[:, cols] = run_sum[:, cols] * alpha + total
                out_acc[:, cols] = out_acc[:, cols] * alpha + mixed

    c_rows = pl.multiple_of(c * BLOCK, BLOCK)
    o_rows = pl.multiple_of((1 - c) * BLOCK, BLOCK)
    forward(kv[0, c, 0], kv[0, c, 1].T, 0, [(0, c_rows, c, None)], True)

    kv_wait(8)
    special_copy().start()
    for e in range(5, 8):
        @pl.when((y + e >= 8) & (column >= 2))
        def _():
            kv_copy(e, True).start()

    kv_wait(1)
    p_copy(1).start()
    for h in range(HEADS):
        g_copies[h].wait()
        gt[h] = g_in[h].T

    def forward_step(e, carry):
        @pl.when(e < 7)
        def _():
            kv_wait(e + 1)
            p_copy(e + 1).start()

        remote(kv.at[e, c], kv.at[e, 1 - c], p_send.at[e], p_recv.at[e], partner).wait_recv()
        keys = kv[e, :, 0].reshape(2 * BLOCK, HEAD_DIM)
        values_t = kv[e, :, 1].reshape(2 * BLOCK, HEAD_DIM).T
        base = p - c - 2 * e
        forward(keys, values_t, e, [(0, 0, 0, bias_of(base)), (BLOCK, BLOCK, 1, bias_of(base + 1))], False)
        return carry

    lax.fori_loop(1, 8, forward_step, 0)

    special_copy().wait_recv()
    special_at = jnp.where(c == 0, p - 15, p - 1)
    forward(kv[0, 1 - c, 0], kv[0, 1 - c, 1].T, 0, [(0, o_rows, 1 - c, bias_of(special_at))], False)

    for h in range(HEADS):
        cols = head_cols(h)
        inv = 1.0 / run_sum[:, cols]
        att_t = (out_acc[:, cols] * inv).astype(jnp.bfloat16)
        att_out[h] = att_t.T
        delta[:, cols] = jnp.sum(
            att_t.astype(jnp.float32) * gt[h].astype(jnp.float32), axis=0, keepdims=True)
        run_sum[:, cols] = inv

    dq_acc[...] = jnp.zeros_like(dq_acc)

    def backward(e):
        keys_t = kv[e, :, 0].reshape(2 * BLOCK, HEAD_DIM).T
        values = kv[e, :, 1].reshape(2 * BLOCK, HEAD_DIM)
        for h in range(HEADS):
            cols = head_cols(h)
            gp = dot_nn(values, gt[h]) - delta[:, cols]
            for parity in (0, 1):
                rows = slice(parity * BLOCK, (parity + 1) * BLOCK)
                factor = jnp.exp2(maxes[e, parity, :, cols] - run_max[:, cols]) * run_sum[:, cols]
                w = probs[e, h, rows].astype(jnp.float32) * factor
                w_scr[h, rows] = w.astype(jnp.bfloat16)
                ds_scr[h, rows] = (w * gp[rows]).astype(jnp.bfloat16)
        ds = side_by_side(ds_scr)
        dk_t = dot_nt(side_by_side(qt), ds)
        dv_t = dot_nt(side_by_side(gt), side_by_side(w_scr))
        for parity in (0, 1):
            rows = slice(parity * BLOCK, (parity + 1) * BLOCK)
            pg[e, parity, 0] = dk_t[:, rows].astype(jnp.bfloat16)
            pg[e, parity, 1] = dv_t[:, rows].astype(jnp.bfloat16)
        dq_acc[...] += dot_nn(keys_t, ds)

    def r1_copy(e):
        return remote(pg.at[e, 1 - c], r1r.at[e], r1_send.at[e], r1_recv.at[e], partner)

    def r2_copy(e):
        passed = jnp.where(e > y + 4, 16, 0)
        return remote(r2s.at[e], r2r.at[e], r2_send.at[e], r2_recv.at[e], seq_dev(passed - 2 * e))

    def chip_sum(e):
        r1_copy(e).wait_recv()
        return pg[e, c].astype(jnp.float32) + r1r[e].astype(jnp.float32)

    def pass_on(e):
        r2s[e] = chip_sum(e).astype(jnp.bfloat16)

        @pl.when(there(-e))
        def _():
            r2_copy(e).start()

    def backward_step(j, carry):
        e = 7 - j
        backward(e)
        r1_copy(e).start()

        @pl.when(j > 0)
        def _():
            pass_on(e + 1)

        return carry

    lax.fori_loop(0, 8, backward_step, 0)

    for h in range(HEADS):
        cols = head_cols(h)
        dq_out[h] = (dq_acc[:, cols] * SCALE).astype(jnp.bfloat16).T

    def r3_copy():
        return remote(r3b, r3r, r3_send, r3_recv, seq_dev(-16))

    own = pg[0, c].astype(jnp.float32)
    r1_copy(0).wait_recv()
    special = r1r[0].astype(jnp.float32)
    own = own + jnp.where(c == 0, special, 0.0)
    r3s[...] = jnp.where(c == 0, 0.0, special)
    for e in range(5, 8):
        @pl.when((y + e >= 8) & (column >= 2))
        def _():
            r2_copy(e).wait_recv()
            r3s[...] += r2r[e].astype(jnp.float32)

    r3b[...] = r3s[...].astype(jnp.bfloat16)

    @pl.when(there(-8))
    def _():
        r3_copy().start()

    total[...] = own
    for e in range(7, 0, -1):
        @pl.when(straight(e) & there(e))
        def _():
            r2_copy(e).wait_recv()
            total[...] += r2r[e].astype(jnp.float32)

    special_copy().wait_send()
    @pl.when(there(8))
    def _():
        kv_copy(8, False).wait_send()

    for e in range(1, 8):
        p_copy(e).wait_send()

        @pl.when(straight(e) & there(e) | (y + e >= 8) & (column >= 2))
        def _():
            kv_copy(e, False).wait_send()

        @pl.when(there(-e))
        def _():
            r2_copy(e).wait_send()

    for e in range(8):
        r1_copy(e).wait_send()


    @pl.when(there(8))
    def _():
        r3_copy().wait_recv()
        total[...] += r3r[...].astype(jnp.float32)

    dkv_out[0] = (total[0] * SCALE).T.astype(jnp.bfloat16)
    dkv_out[1] = total[1].T.astype(jnp.bfloat16)

    @pl.when(there(-8))
    def _():
        r3_copy().wait_send()


def write_out(att, dq, dkv, att_hbm, dq_hbm, dk_hbm, dv_hbm, att_sem, dq_sem, dkv_sem):
    copies = []
    for h in range(HEADS):
        copies.append(pltpu.make_async_copy(att.at[h], att_hbm.at[:, head_cols(h)], att_sem.at[h]))
        copies.append(pltpu.make_async_copy(dq.at[h], dq_hbm.at[:, head_cols(h)], dq_sem.at[h]))
    copies.append(pltpu.make_async_copy(dkv.at[0], dk_hbm, dkv_sem.at[0]))
    copies.append(pltpu.make_async_copy(dkv.at[1], dv_hbm, dkv_sem.at[1]))
    for copy in copies:
        copy.start()
    for copy in copies:
        copy.wait()


def local(queries, key_rows, value_rows, out_grad, doc_ids):
    bf16, f32 = jnp.bfloat16, jnp.float32
    dma = pltpu.SemaphoreType.DMA
    any_space = pl.BlockSpec(memory_space=pl.ANY)
    pair = (2, BLOCK, HEAD_DIM)
    by_head = (HEADS, BLOCK, HEAD_DIM)
    att, dq, dkv = pl.pallas_call(
        kernel,
        out_shape=(pltpu.VMEM(by_head, bf16), pltpu.VMEM(by_head, bf16), pltpu.VMEM(pair, bf16)),
        in_specs=[any_space] * 5,
        out_specs=(pl.BlockSpec(memory_space=pltpu.VMEM),) * 3,
        scratch_shapes=[
            pltpu.VMEM((9, 2) + pair, bf16),
            pltpu.VMEM((HEADS, BLOCK, HEAD_DIM), bf16),
            pltpu.VMEM((HEADS, BLOCK, HEAD_DIM), bf16),
            pltpu.VMEM((HEADS, HEAD_DIM, BLOCK), bf16),
            pltpu.VMEM((HEADS, HEAD_DIM, BLOCK), bf16),
            pltpu.VMEM((8, HEADS, 2 * BLOCK, BLOCK), bf16),
            pltpu.VMEM((8, 2, 1, WIDE), f32),
            pltpu.VMEM((1, WIDE), f32),
            pltpu.VMEM((1, WIDE), f32),
            pltpu.VMEM((HEAD_DIM, WIDE), f32),
            pltpu.VMEM((HEAD_DIM, WIDE), f32),
            pltpu.VMEM((1, WIDE), f32),
            pltpu.VMEM((HEADS, 2 * BLOCK, BLOCK), bf16),
            pltpu.VMEM((HEADS, 2 * BLOCK, BLOCK), bf16),
            pltpu.VMEM((8, 2) + pair, bf16),
            pltpu.VMEM((8,) + pair, bf16),
            pltpu.VMEM((8,) + pair, bf16),
            pltpu.VMEM((8,) + pair, bf16),
            pltpu.VMEM(pair, f32),
            pltpu.VMEM(pair, bf16),
            pltpu.VMEM(pair, bf16),
            pltpu.VMEM(pair, f32),
            pltpu.SMEM((NBLK,), jnp.int32),
            dma((2,)), dma((HEADS,)), dma((HEADS,)),
            dma,
            dma((9,)), dma((9,)), dma((8,)), dma((8,)),
            dma((8,)), dma((8,)), dma((8,)), dma((8,)), dma, dma,
        ],
        compiler_params=pltpu.CompilerParams(collective_id=0, has_side_effects=True),
    )(queries, key_rows, value_rows, out_grad, doc_ids)
    wide = jax.ShapeDtypeStruct((BLOCK, WIDE), bf16)
    narrow = jax.ShapeDtypeStruct((BLOCK, HEAD_DIM), bf16)
    return pl.pallas_call(
        write_out,
        out_shape=(wide, wide, narrow, narrow),
        in_specs=[pl.BlockSpec(memory_space=pltpu.VMEM)] * 3,
        out_specs=(any_space,) * 4,
        scratch_shapes=[dma((HEADS,)), dma((HEADS,)), dma((2,))],
        compiler_params=pltpu.CompilerParams(vmem_limit_bytes=1 << 20),
    )(*[pltpu.with_memory_space_constraint(out, pltpu.VMEM) for out in (att, dq, dkv)])


def solution(mesh):
    rows = P(("pb", "kv"), None)
    return jax.shard_map(
        local, mesh=mesh, in_specs=(rows, rows, rows, rows, P()),
        out_specs=(rows, rows, rows, rows), check_vma=False)
```

time: 45.3 us -> 40.7 us (0.90)
  the two profiles are of different devices: /device:TPU:8 before, /device:TPU:101 now
where the time goes in v2:
time: 40.7 us; the launch traced here: 40.5 us
  Pallas kernels  39.9 us (98%)
  between operations  0.64 us (2%)
    pallas_call x1, Pallas kernels, local(): pl.pallas_call(kernel, out_shape=(pltpu.VMEM(by_head, bf16), pltpu.VMEM(b...  38.9 us
    pallas_call x1, Pallas kernels, local(): pl.pallas_call(write_out, out_shape=(wide, wide, narrow, narrow), in_spec...  0.96 us

profile of v2, /device:TPU:101, one launch (start us, length us, event | category | flops | bytes accessed | tf_op | source)
XLA Modules:
  0.0 40.5 jit_solution(14764138829074284508)
XLA Ops:
  0.6 38.9 %shard_map.84 = (bf16[8,128,128]{2,1,0:T(8,128)(2,1)S(1)}, bf16[8,128,128]{2,1,0:T(8,128)(2,1)S(1)}, bf16[2,128,128]{2,1,0:T(8,128)(2,1)S(1)}) custom-call(bf16[128,1024]{1,0:T(8,128)(2,1)} %q_hbm.1, bf16[128,128]{1,0:T(8,128)(2,1)} %k_hbm.1, bf16[128,128]{1,0:T(8,128)(2,1)} %v_hbm.1, bf16[128,1024]{1,0:T(8,128)(2,1)} %g_hbm.1, s32[256]{0:T(256)} %docs_hbm.1), custom_call_target="tpu_custom_call" | custom-call | tf_op jit(solution)/shard_map/pallas_call | solution.py:361
  39.6 1.0 %shard_map.85 = (bf16[128,1024]{1,0:T(8,128)(2,1)}, bf16[128,1024]{1,0:T(8,128)(2,1)}, bf16[128,128]{1,0:T(8,128)(2,1)}, bf16[128,128]{1,0:T(8,128)(2,1)}) custom-call(bf16[8,128,128]{2,1,0:T(8,128)(2,1)S(1)} %get-tuple-element.7.att, bf16[8,128,128]{2,1,0:T(8,128)(2,1)S(1)} %get-tuple-element.8.dq, bf16[2,128,128]{2,1,0:T(8,128)(2,1)S(1)} %get-tuple-element.9.dkv), custom_call_target="tpu_custom_call" | custom-call | tf_op jit(solution)/shard_map/pallas_call | solution.py:399

commit v3 on v2

--- a/solution.py
+++ b/solution.py
@@ -40,10 +40,10 @@
     q_hbm, k_hbm, v_hbm, g_hbm, docs_hbm,
     att_out, dq_out, dkv_out,
     kv, q_in, g_in, qt, gt, probs, maxes, run_max, run_sum, out_acc, dq_acc, delta,
-    w_scr, ds_scr, pg, r1r, r2s, r2r, r3s, r3b, r3r, total, docs,
+    w_a, ds_a, w_b, ds_b, ds_all, pg, r1r, r2s, r2r, r3s, r3b, r3r, one_back, r4b, r4r, total, docs,
     local_sem, q_sem, g_sem, docs_sem,
     kv_send, kv_recv, p_send, p_recv,
-    r1_send, r1_recv, r2_send, r2_recv, r3_send, r3_recv,
+    r1_send, r1_recv, r2_send, r2_recv, r3_send, r3_recv, r4_send, r4_recv,
 ):
     pb = lax.axis_index("pb")
     kvi = lax.axis_index("kv")
@@ -117,7 +117,15 @@
     def special_copy():
         return remote(kv.at[8 * c, c], kv.at[0, c], p_send.at[0], p_recv.at[0], partner)
 
-    @pl.when(there(8))
+    two_on = there(8) & ((y > 0) | (c == 1))
+    two_back = there(-8) & ((y > 0) | (c == 1))
+
+    def two_wait():
+        @pl.when(two_back)
+        def _():
+            remote(kv.at[0, c], kv.at[8, c], kv_send.at[8], kv_recv.at[8], partner).wait_recv()
+
+    @pl.when(two_on & (y > 0))
     def _():
         kv_copy(8, False).start()
 
@@ -125,6 +133,14 @@
         @pl.when(straight(e) & there(e))
         def _():
             kv_copy(e, False).start()
+
+    @pl.when(two_on & (y == 0))
+    def _():
+        kv_copy(8, False).start()
+
+    @pl.when(c == 0)
+    def _():
+        special_copy().start()
 
     for h in range(HEADS):
         q_copies[h].wait()
@@ -180,24 +196,39 @@
     o_rows = pl.multiple_of((1 - c) * BLOCK, BLOCK)
     forward(kv[0, c, 0], kv[0, c, 1].T, 0, [(0, c_rows, c, None)], True)
 
-    kv_wait(8)
-    special_copy().start()
+    @pl.when(y > 0)
+    def _():
+        two_wait()
+
+        @pl.when(c == 1)
+        def _():
+            special_copy().start()
+
     for e in range(5, 8):
         @pl.when((y + e >= 8) & (column >= 2))
         def _():
             kv_copy(e, True).start()
 
-    kv_wait(1)
-    p_copy(1).start()
+    for e in (1, 2):
+        kv_wait(e)
+        p_copy(e).start()
     for h in range(HEADS):
         g_copies[h].wait()
         gt[h] = g_in[h].T
 
     def forward_step(e, carry):
-        @pl.when(e < 7)
-        def _():
-            kv_wait(e + 1)
-            p_copy(e + 1).start()
+        @pl.when(e < 6)
+        def _():
+            kv_wait(e + 2)
+            p_copy(e + 2).start()
+
+        @pl.when((e == 5) & (y == 0))
+        def _():
+            two_wait()
+
+            @pl.when(c == 1)
+            def _():
+                special_copy().start()
 
         remote(kv.at[e, c], kv.at[e, 1 - c], p_send.at[e], p_recv.at[e], partner).wait_recv()
         keys = kv[e, :, 0].reshape(2 * BLOCK, HEAD_DIM)
@@ -221,10 +252,7 @@
             att_t.astype(jnp.float32) * gt[h].astype(jnp.float32), axis=0, keepdims=True)
         run_sum[:, cols] = inv
 
-    dq_acc[...] = jnp.zeros_like(dq_acc)
-
-    def backward(e):
-        keys_t = kv[e, :, 0].reshape(2 * BLOCK, HEAD_DIM).T
+    def weigh(e, w_scr, ds_scr):
         values = kv[e, :, 1].reshape(2 * BLOCK, HEAD_DIM)
         for h in range(HEADS):
             cols = head_cols(h)
@@ -234,80 +262,148 @@
                 factor = jnp.exp2(maxes[e, parity, :, cols] - run_max[:, cols]) * run_sum[:, cols]
                 w = probs[e, h, rows].astype(jnp.float32) * factor
                 w_scr[h, rows] = w.astype(jnp.bfloat16)
-                ds_scr[h, rows] = (w * gp[rows]).astype(jnp.bfloat16)
-        ds = side_by_side(ds_scr)
-        dk_t = dot_nt(side_by_side(qt), ds)
+                ds = (w * gp[rows]).astype(jnp.bfloat16)
+                ds_scr[h, rows] = ds
+                ds_all[e, h, rows] = ds
+
+    def products(e, w_scr, ds_scr):
+        dk_t = dot_nt(side_by_side(qt), side_by_side(ds_scr))
         dv_t = dot_nt(side_by_side(gt), side_by_side(w_scr))
         for parity in (0, 1):
             rows = slice(parity * BLOCK, (parity + 1) * BLOCK)
             pg[e, parity, 0] = dk_t[:, rows].astype(jnp.bfloat16)
             pg[e, parity, 1] = dv_t[:, rows].astype(jnp.bfloat16)
-        dq_acc[...] += dot_nn(keys_t, ds)
 
     def r1_copy(e):
         return remote(pg.at[e, 1 - c], r1r.at[e], r1_send.at[e], r1_recv.at[e], partner)
 
+    def r3_copy():
+        return remote(r3b, r3r, r3_send, r3_recv, seq_dev(-16))
+
+    def beside(e):
+        return (e == 3) & (y < 3) | (e == 5) & (y > 0) | (e == 7) & (y == 3) | (e == 1) & (y == 0)
+
     def r2_copy(e):
-        passed = jnp.where(e > y + 4, 16, 0)
+        passed = jnp.where(beside(e), 8, jnp.where(e > y + 4, 16, 0))
         return remote(r2s.at[e], r2r.at[e], r2_send.at[e], r2_recv.at[e], seq_dev(passed - 2 * e))
 
     def chip_sum(e):
         r1_copy(e).wait_recv()
         return pg[e, c].astype(jnp.float32) + r1r[e].astype(jnp.float32)
 
+    def r4_copy():
+        return remote(r4b, r4r, r4_send, r4_recv, seq_dev(-8))
+
     def pass_on(e):
-        r2s[e] = chip_sum(e).astype(jnp.bfloat16)
-
-        @pl.when(there(-e))
-        def _():
-            r2_copy(e).start()
-
-    def backward_step(j, carry):
-        e = 7 - j
-        backward(e)
-        r1_copy(e).start()
-
-        @pl.when(j > 0)
-        def _():
-            pass_on(e + 1)
-
+        @pl.when(e != 4)
+        def _():
+            r2s[e] = chip_sum(e).astype(jnp.bfloat16)
+
+            @pl.when(there(-e))
+            def _():
+                r2_copy(e).start()
+
+    orders = [(0, 3, 1, 7, 6, 5, 4, 2), (0, 3, 5, 7, 6, 4, 2, 1), (0, 3, 5, 7, 4, 6, 2, 1), (0, 5, 7, 4, 6, 2, 3, 1)]
+    codes = [sum(e << (3 * j) for j, e in enumerate(order)) for order in orders]
+    turns = jnp.where(y == 0, codes[0], jnp.where(y == 1, codes[1], jnp.where(y == 2, codes[2], codes[3])))
+
+    def turn(j):
+        return lax.rem(lax.shift_right_logical(turns, 3 * jnp.asarray(j, jnp.int32)), 8)
+
+    later_sum = y > 0
+    beside_in = {1: y == 3, 3: y > 0, 5: y < 3, 7: y == 0}
+    straight_in = {
+        e: (y + e < 4) | there(e) & ((e == 6) & (y < 2) | (e == 2) & (y > 1)) for e in (1, 2, 3, 6)}
+    r3_sent = there(-8) & ((y > 0) | (c == 1))
+    r3_due = there(8) & ((y > 0) | (c == 1))
+
+    def hand_over(j):
+        r1_copy(turn(j)).start()
+
+        @pl.when(j > 2)
+        def _():
+            pass_on(turn(j - 2))
+
+        @pl.when((j == 2) & ~later_sum)
+        def _():
+            r1_copy(0).wait_recv()
+            special = r1r[0].astype(jnp.float32)
+            total[...] = pg[0, c].astype(jnp.float32) + jnp.where(c == 0, special, 0.0)
+
+            @pl.when(there(-8) & (c == 1))
+            def _():
+                r3b[...] = r1r[0]
+                r3_copy().start()
+
+    weigh(turn(0), w_a, ds_a)
+
+    def backward_steps(i, carry):
+        j = 2 * i
+        weigh(turn(j + 1), w_b, ds_b)
+        products(turn(j), w_a, ds_a)
+        hand_over(j)
+        weigh(turn(j + 2), w_a, ds_a)
+        products(turn(j + 1), w_b, ds_b)
+        hand_over(j + 1)
         return carry
 
-    lax.fori_loop(0, 8, backward_step, 0)
-
-    for h in range(HEADS):
-        cols = head_cols(h)
-        dq_out[h] = (dq_acc[:, cols] * SCALE).astype(jnp.bfloat16).T
-
-    def r3_copy():
-        return remote(r3b, r3r, r3_send, r3_recv, seq_dev(-16))
-
-    own = pg[0, c].astype(jnp.float32)
-    r1_copy(0).wait_recv()
-    special = r1r[0].astype(jnp.float32)
-    own = own + jnp.where(c == 0, special, 0.0)
-    r3s[...] = jnp.where(c == 0, 0.0, special)
+    lax.fori_loop(0, 3, backward_steps, 0)
+    weigh(turn(7), w_b, ds_b)
+    products(turn(6), w_a, ds_a)
+    hand_over(jnp.int32(6))
+    products(turn(7), w_b, ds_b)
+    hand_over(jnp.int32(7))
+    pass_on(turn(6))
+    pass_on(turn(7))
+
+    one_back[...] = chip_sum(4)
+    for e in (1, 3, 5, 7):
+        @pl.when(beside_in[e] & (column >= 1))
+        def _():
+            r2_copy(e).wait_recv()
+            one_back[...] += r2r[e].astype(jnp.float32)
+
+    @pl.when(there(-4))
+    def _():
+        r4b[...] = one_back[...].astype(jnp.bfloat16)
+        r4_copy().start()
+
+    @pl.when(later_sum)
+    def _():
+        r1_copy(0).wait_recv()
+        special = r1r[0].astype(jnp.float32)
+        total[...] = pg[0, c].astype(jnp.float32) + jnp.where(c == 0, special, 0.0)
+        r3s[...] = jnp.where(c == 0, 0.0, special)
+
     for e in range(5, 8):
         @pl.when((y + e >= 8) & (column >= 2))
         def _():
             r2_copy(e).wait_recv()
             r3s[...] += r2r[e].astype(jnp.float32)
 
-    r3b[...] = r3s[...].astype(jnp.bfloat16)
-
-    @pl.when(there(-8))
-    def _():
+    @pl.when(there(-8) & (y > 0))
+    def _():
+        r3b[...] = r3s[...].astype(jnp.bfloat16)
         r3_copy().start()
 
-    total[...] = own
-    for e in range(7, 0, -1):
-        @pl.when(straight(e) & there(e))
+    def query_grads(e, carry):
+        keys_t = kv[e, :, 0].reshape(2 * BLOCK, HEAD_DIM).T
+        dq_acc[...] += dot_nn(keys_t, side_by_side(ds_all.at[e]))
+        return carry
+
+    dq_acc[...] = dot_nn(kv[0, :, 0].reshape(2 * BLOCK, HEAD_DIM).T, side_by_side(ds_all.at[0]))
+    lax.fori_loop(1, 8, query_grads, 0)
+    for h in range(HEADS):
+        dq_out[h] = (dq_acc[:, head_cols(h)] * SCALE).astype(jnp.bfloat16).T
+
+    for e in (6, 3, 2, 1):
+        @pl.when(straight_in[e])
         def _():
             r2_copy(e).wait_recv()
             total[...] += r2r[e].astype(jnp.float32)
 
     special_copy().wait_send()
-    @pl.when(there(8))
+    @pl.when(two_on)
     def _():
         kv_copy(8, False).wait_send()
 
@@ -318,15 +414,21 @@
         def _():
             kv_copy(e, False).wait_send()
 
-        @pl.when(there(-e))
-        def _():
-            r2_copy(e).wait_send()
+        if e != 4:
+            @pl.when(there(-e))
+            def _():
+                r2_copy(e).wait_send()
 
     for e in range(8):
         r1_copy(e).wait_send()
 
 
-    @pl.when(there(8))
+    @pl.when(there(4))
+    def _():
+        r4_copy().wait_recv()
+        total[...] += r4r[...].astype(jnp.float32)
+
+    @pl.when(r3_due)
     def _():
         r3_copy().wait_recv()
         total[...] += r3r[...].astype(jnp.float32)
@@ -334,9 +436,13 @@
     dkv_out[0] = (total[0] * SCALE).T.astype(jnp.bfloat16)
     dkv_out[1] = total[1].T.astype(jnp.bfloat16)
 
-    @pl.when(there(-8))
+    @pl.when(r3_sent)
     def _():
         r3_copy().wait_send()
+
+    @pl.when(there(-4))
+    def _():
+        r4_copy().wait_send()
 
 
 def write_out(att, dq, dkv, att_hbm, dq_hbm, dk_hbm, dv_hbm, att_sem, dq_sem, dkv_sem):
@@ -378,6 +484,9 @@
             pltpu.VMEM((1, WIDE), f32),
             pltpu.VMEM((HEADS, 2 * BLOCK, BLOCK), bf16),
             pltpu.VMEM((HEADS, 2 * BLOCK, BLOCK), bf16),
+            pltpu.VMEM((HEADS, 2 * BLOCK, BLOCK), bf16),
+            pltpu.VMEM((HEADS, 2 * BLOCK, BLOCK), bf16),
+            pltpu.VMEM((8, HEADS, 2 * BLOCK, BLOCK), bf16),
             pltpu.VMEM((8, 2) + pair, bf16),
             pltpu.VMEM((8,) + pair, bf16),
             pltpu.VMEM((8,) + pair, bf16),
@@ -386,11 +495,14 @@
             pltpu.VMEM(pair, bf16),
             pltpu.VMEM(pair, bf16),
             pltpu.VMEM(pair, f32),
+            pltpu.VMEM(pair, bf16),
+            pltpu.VMEM(pair, bf16),
+            pltpu.VMEM(pair, f32),
             pltpu.SMEM((NBLK,), jnp.int32),
             dma((2,)), dma((HEADS,)), dma((HEADS,)),
             dma,
             dma((9,)), dma((9,)), dma((8,)), dma((8,)),
-            dma((8,)), dma((8,)), dma((8,)), dma((8,)), dma, dma,
+            dma((8,)), dma((8,)), dma((8,)), dma((8,)), dma, dma, dma, dma,
         ],
         compiler_params=pltpu.CompilerParams(collective_id=0, has_side_effects=True),
     )(queries, key_rows, value_rows, out_grad, doc_ids)

time: 40.7 us -> 39.2 us (0.963)
  the two profiles are of different devices: /device:TPU:101 before, /device:TPU:124 now
where the time goes in v3:
time: 39.2 us; the launch traced here: 39 us
  Pallas kernels  38.3 us (98%)
  between operations  0.64 us (2%)
    pallas_call x1, Pallas kernels, local(): pl.pallas_call(kernel, out_shape=(pltpu.VMEM(by_head, bf16), pltpu.VMEM(b...  37.4 us
    pallas_call x1, Pallas kernels, local(): pl.pallas_call(write_out, out_shape=(wide, wide, narrow, narrow), in_spec...  0.96 us

profile of v3, /device:TPU:124, one launch (start us, length us, event | category | flops | bytes accessed | tf_op | source)
XLA Modules:
  0.0 39.0 jit_solution(4501368083220549986)
XLA Ops:
  0.6 37.4 %shard_map.84 = (bf16[8,128,128]{2,1,0:T(8,128)(2,1)S(1)}, bf16[8,128,128]{2,1,0:T(8,128)(2,1)S(1)}, bf16[2,128,128]{2,1,0:T(8,128)(2,1)S(1)}) custom-call(bf16[128,1024]{1,0:T(8,128)(2,1)} %q_hbm.1, bf16[128,128]{1,0:T(8,128)(2,1)} %k_hbm.1, bf16[128,128]{1,0:T(8,128)(2,1)} %v_hbm.1, bf16[128,1024]{1,0:T(8,128)(2,1)} %g_hbm.1, s32[256]{0:T(256)} %docs_hbm.1), custom_call_target="tpu_custom_call" | custom-call | tf_op jit(solution)/shard_map/pallas_call | solution.py:467
  38.0 1.0 %shard_map.85 = (bf16[128,1024]{1,0:T(8,128)(2,1)}, bf16[128,1024]{1,0:T(8,128)(2,1)}, bf16[128,128]{1,0:T(8,128)(2,1)}, bf16[128,128]{1,0:T(8,128)(2,1)}) custom-call(bf16[8,128,128]{2,1,0:T(8,128)(2,1)S(1)} %get-tuple-element.7.att, bf16[8,128,128]{2,1,0:T(8,128)(2,1)S(1)} %get-tuple-element.8.dq, bf16[2,128,128]{2,1,0:T(8,128)(2,1)S(1)} %get-tuple-element.9.dkv), custom_call_target="tpu_custom_call" | custom-call | tf_op jit(solution)/shard_map/pallas_call | solution.py:511

commit v4 on v3

--- a/solution.py
+++ b/solution.py
@@ -303,7 +303,7 @@
             def _():
                 r2_copy(e).start()
 
-    orders = [(0, 3, 1, 7, 6, 5, 4, 2), (0, 3, 5, 7, 6, 4, 2, 1), (0, 3, 5, 7, 4, 6, 2, 1), (0, 5, 7, 4, 6, 2, 3, 1)]
+    orders = [(0, 3, 1, 2, 7, 6, 5, 4), (0, 3, 5, 2, 7, 6, 4, 1), (0, 3, 5, 6, 7, 4, 2, 1), (0, 5, 7, 6, 4, 2, 3, 1)]
     codes = [sum(e << (3 * j) for j, e in enumerate(order)) for order in orders]
     turns = jnp.where(y == 0, codes[0], jnp.where(y == 1, codes[1], jnp.where(y == 2, codes[2], codes[3])))
 

time: 39.2 us -> 38.5 us (0.982)
  Pallas kernels: 38.3 us -> 37.5 us
    pallas_call x1, Pallas kernels: 37.4 us -> 36.6 us  [local(): pl.pallas_call(kernel, out_shape=(pltpu.VMEM(by_head, bf16), pltpu.VMEM(b...]
where the time goes in v4:
time: 38.5 us; the launch traced here: 38.2 us
  Pallas kernels  37.5 us (97%)
  between operations  0.64 us (2%)
    pallas_call x1, Pallas kernels, local(): pl.pallas_call(kernel, out_shape=(pltpu.VMEM(by_head, bf16), pltpu.VMEM(b...  36.6 us
    pallas_call x1, Pallas kernels, local(): pl.pallas_call(write_out, out_shape=(wide, wide, narrow, narrow), in_spec...  0.96 us

profile of v4, /device:TPU:124, one launch (start us, length us, event | category | flops | bytes accessed | tf_op | source)
XLA Modules:
  0.0 38.2 jit_solution(11749400786648669340)
XLA Ops:
  0.6 36.6 %shard_map.84 = (bf16[8,128,128]{2,1,0:T(8,128)(2,1)S(1)}, bf16[8,128,128]{2,1,0:T(8,128)(2,1)S(1)}, bf16[2,128,128]{2,1,0:T(8,128)(2,1)S(1)}) custom-call(bf16[128,1024]{1,0:T(8,128)(2,1)} %q_hbm.1, bf16[128,128]{1,0:T(8,128)(2,1)} %k_hbm.1, bf16[128,128]{1,0:T(8,128)(2,1)} %v_hbm.1, bf16[128,1024]{1,0:T(8,128)(2,1)} %g_hbm.1, s32[256]{0:T(256)} %docs_hbm.1), custom_call_target="tpu_custom_call" | custom-call | tf_op jit(solution)/shard_map/pallas_call | solution.py:467
  37.2 1.0 %shard_map.85 = (bf16[128,1024]{1,0:T(8,128)(2,1)}, bf16[128,1024]{1,0:T(8,128)(2,1)}, bf16[128,128]{1,0:T(8,128)(2,1)}, bf16[128,128]{1,0:T(8,128)(2,1)}) custom-call(bf16[8,128,128]{2,1,0:T(8,128)(2,1)S(1)} %get-tuple-element.7.att, bf16[8,128,128]{2,1,0:T(8,128)(2,1)S(1)} %get-tuple-element.8.dq, bf16[2,128,128]{2,1,0:T(8,128)(2,1)S(1)} %get-tuple-element.9.dkv), custom_call_target="tpu_custom_call" | custom-call | tf_op jit(solution)/shard_map/pallas_call | solution.py:511

commit v5 on v4

--- a/solution.py
+++ b/solution.py
@@ -303,7 +303,7 @@
             def _():
                 r2_copy(e).start()
 
-    orders = [(0, 3, 1, 2, 7, 6, 5, 4), (0, 3, 5, 2, 7, 6, 4, 1), (0, 3, 5, 6, 7, 4, 2, 1), (0, 5, 7, 6, 4, 2, 3, 1)]
+    orders = [(0, 2, 3, 1, 7, 6, 5, 4), (0, 2, 3, 5, 7, 6, 4, 1), (0, 6, 3, 5, 7, 4, 2, 1), (0, 6, 5, 7, 4, 2, 3, 1)]
     codes = [sum(e << (3 * j) for j, e in enumerate(order)) for order in orders]
     turns = jnp.where(y == 0, codes[0], jnp.where(y == 1, codes[1], jnp.where(y == 2, codes[2], codes[3])))
 

time: 38.5 us -> 38.3 us (level)
  no operation moved by 1% of the time
where the time goes in v5:
time: 38.3 us; the launch traced here: 38.1 us
  Pallas kernels  37.5 us (98%)
  between operations  0.64 us (2%)
    pallas_call x1, Pallas kernels, local(): pl.pallas_call(kernel, out_shape=(pltpu.VMEM(by_head, bf16), pltpu.VMEM(b...  36.5 us
    pallas_call x1, Pallas kernels, local(): pl.pallas_call(write_out, out_shape=(wide, wide, narrow, narrow), in_spec...  0.96 us

profile of v5, /device:TPU:124, one launch (start us, length us, event | category | flops | bytes accessed | tf_op | source)
XLA Modules:
  0.0 38.1 jit_solution(9297440622681875250)
XLA Ops:
  0.6 36.5 %shard_map.84 = (bf16[8,128,128]{2,1,0:T(8,128)(2,1)S(1)}, bf16[8,128,128]{2,1,0:T(8,128)(2,1)S(1)}, bf16[2,128,128]{2,1,0:T(8,128)(2,1)S(1)}) custom-call(bf16[128,1024]{1,0:T(8,128)(2,1)} %q_hbm.1, bf16[128,128]{1,0:T(8,128)(2,1)} %k_hbm.1, bf16[128,128]{1,0:T(8,128)(2,1)} %v_hbm.1, bf16[128,1024]{1,0:T(8,128)(2,1)} %g_hbm.1, s32[256]{0:T(256)} %docs_hbm.1), custom_call_target="tpu_custom_call" | custom-call | tf_op jit(solution)/shard_map/pallas_call | solution.py:467
  37.2 1.0 %shard_map.85 = (bf16[128,1024]{1,0:T(8,128)(2,1)}, bf16[128,1024]{1,0:T(8,128)(2,1)}, bf16[128,128]{1,0:T(8,128)(2,1)}, bf16[128,128]{1,0:T(8,128)(2,1)}) custom-call(bf16[8,128,128]{2,1,0:T(8,128)(2,1)S(1)} %get-tuple-element.7.att, bf16[8,128,128]{2,1,0:T(8,128)(2,1)S(1)} %get-tuple-element.8.dq, bf16[2,128,128]{2,1,0:T(8,128)(2,1)S(1)} %get-tuple-element.9.dkv), custom_call_target="tpu_custom_call" | custom-call | tf_op jit(solution)/shard_map/pallas_call | solution.py:511

commit v6 on v5

--- a/solution.py
+++ b/solution.py
@@ -40,7 +40,7 @@
     q_hbm, k_hbm, v_hbm, g_hbm, docs_hbm,
     att_out, dq_out, dkv_out,
     kv, q_in, g_in, qt, gt, probs, maxes, run_max, run_sum, out_acc, dq_acc, delta,
-    w_a, ds_a, w_b, ds_b, ds_all, pg, r1r, r2s, r2r, r3s, r3b, r3r, one_back, r4b, r4r, total, docs,
+    w_a, ds_a, w_b, ds_b, ds_all, att_ts, pg, r1r, r2s, r2r, r3s, r3b, r3r, one_back, r4b, r4r, total, docs,
     local_sem, q_sem, g_sem, docs_sem,
     kv_send, kv_recv, p_send, p_recv,
     r1_send, r1_recv, r2_send, r2_recv, r3_send, r3_recv, r4_send, r4_recv,
@@ -68,7 +68,7 @@
             kv[e, c] = jnp.zeros((2, BLOCK, HEAD_DIM), jnp.bfloat16)
 
     barrier = pltpu.get_barrier_semaphore()
-    peers = [e for d in range(1, 9) for e in (d, -d)]
+    peers = [e for d in range(8, 0, -1) for e in (d, -d)]
     count = jnp.int32(1)
     pl.semaphore_signal(barrier, inc=1, device_id=partner, device_id_type=MESH)
     for e in peers:
@@ -247,7 +247,7 @@
         cols = head_cols(h)
         inv = 1.0 / run_sum[:, cols]
         att_t = (out_acc[:, cols] * inv).astype(jnp.bfloat16)
-        att_out[h] = att_t.T
+        att_ts[h] = att_t
         delta[:, cols] = jnp.sum(
             att_t.astype(jnp.float32) * gt[h].astype(jnp.float32), axis=0, keepdims=True)
         run_sum[:, cols] = inv
@@ -394,6 +394,7 @@
     dq_acc[...] = dot_nn(kv[0, :, 0].reshape(2 * BLOCK, HEAD_DIM).T, side_by_side(ds_all.at[0]))
     lax.fori_loop(1, 8, query_grads, 0)
     for h in range(HEADS):
+        att_out[h] = att_ts[h].T
         dq_out[h] = (dq_acc[:, head_cols(h)] * SCALE).astype(jnp.bfloat16).T
 
     for e in (6, 3, 2, 1):
@@ -487,6 +488,7 @@
             pltpu.VMEM((HEADS, 2 * BLOCK, BLOCK), bf16),
             pltpu.VMEM((HEADS, 2 * BLOCK, BLOCK), bf16),
             pltpu.VMEM((8, HEADS, 2 * BLOCK, BLOCK), bf16),
+            pltpu.VMEM((HEADS, HEAD_DIM, BLOCK), bf16),
             pltpu.VMEM((8, 2) + pair, bf16),
             pltpu.VMEM((8,) + pair, bf16),
             pltpu.VMEM((8,) + pair, bf16),

time: 38.3 us -> 38.2 us (level)
  no operation moved by 1% of the time
where the time goes in v6:
time: 38.2 us; the launch traced here: 38.1 us
  Pallas kernels  37.4 us (98%)
  between operations  0.64 us (2%)
    pallas_call x1, Pallas kernels, local(): pl.pallas_call(kernel, out_shape=(pltpu.VMEM(by_head, bf16), pltpu.VMEM(b...  36.5 us
    pallas_call x1, Pallas kernels, local(): pl.pallas_call(write_out, out_shape=(wide, wide, narrow, narrow), in_spec...  0.96 us

profile of v6, /device:TPU:124, one launch (start us, length us, event | category | flops | bytes accessed | tf_op | source)
XLA Modules:
  0.0 38.1 jit_solution(12370381676717270574)
XLA Ops:
  0.6 36.5 %shard_map.84 = (bf16[8,128,128]{2,1,0:T(8,128)(2,1)S(1)}, bf16[8,128,128]{2,1,0:T(8,128)(2,1)S(1)}, bf16[2,128,128]{2,1,0:T(8,128)(2,1)S(1)}) custom-call(bf16[128,1024]{1,0:T(8,128)(2,1)} %q_hbm.1, bf16[128,128]{1,0:T(8,128)(2,1)} %k_hbm.1, bf16[128,128]{1,0:T(8,128)(2,1)} %v_hbm.1, bf16[128,1024]{1,0:T(8,128)(2,1)} %g_hbm.1, s32[256]{0:T(256)} %docs_hbm.1), custom_call_target="tpu_custom_call" | custom-call | tf_op jit(solution)/shard_map/pallas_call | solution.py:468
  37.1 1.0 %shard_map.85 = (bf16[128,1024]{1,0:T(8,128)(2,1)}, bf16[128,1024]{1,0:T(8,128)(2,1)}, bf16[128,128]{1,0:T(8,128)(2,1)}, bf16[128,128]{1,0:T(8,128)(2,1)}) custom-call(bf16[8,128,128]{2,1,0:T(8,128)(2,1)S(1)} %get-tuple-element.7.att, bf16[8,128,128]{2,1,0:T(8,128)(2,1)S(1)} %get-tuple-element.8.dq, bf16[2,128,128]{2,1,0:T(8,128)(2,1)S(1)} %get-tuple-element.9.dkv), custom_call_target="tpu_custom_call" | custom-call | tf_op jit(solution)/shard_map/pallas_call | solution.py:513
